TPU v7x, 256 devices: a whole 4x4x8 slice. The times are simulated.
256 devices in a mesh: dp: 16 (over y_hi, x, core), tensor: 16 (over z, y_lo).
Axes of the slice: x: 4, y: 4 (y_hi: 2, y_lo: 2; y = y_hi * 2 + y_lo), z: 8, core: 2. Of those that a mesh axis runs over, the one named last changes fastest.
Arguments:
- tokens: bfloat16 [8192, 8192], P('dp', 'tensor'), may hold values from -13 to 13
- proj: bfloat16 [8192, 8192], P('tensor'), may hold values from -8 to 8
- gain: float32 [8192], P('tensor'), may hold values from 0.1 to 1.9
- target: bfloat16 [8192, 8192], P('dp', 'tensor'), may hold values from -6 to 6
- adapter_down_weight: bfloat16 [256, 64, 8192], P('dp', None, 'tensor'), may hold values from -0.0625 to 0.0625
- adapter_up_weight: bfloat16 [256, 64, 8192], P('dp', None, 'tensor'), may hold values from -0.75 to 0.75
- source_row_index: int32 [16, 16, 96], P('dp'), may hold values from 0 to 512, as said below
- padded_row_index: int32 [16, 3584], P('dp'), may hold values from 0 to 1536, as said below
- padded_block_tenant: int32 [16, 28], P('dp'), may hold values from 0 to 15, as said below
Outputs:
- draft: bfloat16 [8192, 8192], P('dp', 'tensor')
- grad_down: bfloat16 [256, 64, 8192], P('dp', None, 'tensor')
- grad_up: bfloat16 [256, 64, 8192], P('dp', None, 'tensor')
Inputs may be any that keep to these rules, and one draw needn't show every extreme that they name: For source s and owner d, the first c[s, d] entries of source_row_index[s, d] are rows of source s and the rest are 512; every row of a source appears exactly once over all owners. Some source fills all 96 slots to some owner, and some owner receives 96 rows from every source. `padded_row_index`: for owner d, every live slot s * 96 + j (source_row_index[s, d, j] < 512) appears exactly once, all other entries are 1536; the rows of one block of 128 padded rows belong to one tenant. `padded_block_tenant`: nondecreasing along the blocks of an owner.
All inputs are finite; a program needn't handle non-finite values.
Results may differ from a plain program's by a relative error of at most 0.02.
Values may be sent and summed in bfloat16 or wider, within the bound.
A program may use at most 128 MiB of HBM per device.

v0:
```python
import jax
import jax.numpy as jnp
from jax import lax
from jax.sharding import PartitionSpec as P

MODEL_WIDTH = 8192


def to_padded(values, positions):
    extended = jnp.concatenate([values, jnp.zeros((1, values.shape[1]), values.dtype)])
    return extended[positions]


def body(
    tokens,
    proj,
    gain,
    target,
    adapter_down_weight,
    adapter_up_weight,
    source_row_index,
    padded_row_index,
    padded_block_tenant,
):
    row_count, feat_width = tokens.shape
    dp_count = lax.axis_size("dp")
    slot_cap = source_row_index.shape[2]
    slot_total = dp_count * slot_cap
    routes = source_row_index[0].reshape(slot_total)
    positions = padded_row_index[0]
    local_tenant_index = padded_block_tenant[0]
    block_count = local_tenant_index.shape[0]
    block_rows = positions.shape[0] // block_count
    outgoing = to_padded(tokens, routes).reshape(dp_count, slot_cap, feat_width)
    arrived = lax.all_to_all(outgoing, "dp", split_axis=0, concat_axis=0, tiled=True)
    feat_padded = to_padded(arrived.reshape(slot_total, feat_width), positions).reshape(
        block_count, block_rows, feat_width
    )
    down_weight_tiles = adapter_down_weight[local_tenant_index]
    up_weight_tiles = adapter_up_weight[local_tenant_index]
    rank_part = jnp.einsum(
        "brk,bpk->brp", down_weight_tiles, feat_padded, preferred_element_type=jnp.float32
    )
    rank_act = lax.psum(rank_part.astype(jnp.bfloat16), "tensor")
    delta_pad = (
        2.0
        * jnp.einsum("brp,bro->bpo", rank_act, up_weight_tiles, preferred_element_type=jnp.float32)
    ).astype(jnp.bfloat16)
    delta_slots = (
        jnp.zeros((slot_total + 1, feat_width), jnp.bfloat16)
        .at[positions]
        .set(delta_pad.reshape(-1, feat_width))[:slot_total]
    )
    returned = lax.all_to_all(
        delta_slots.reshape(dp_count, slot_cap, feat_width),
        "dp",
        split_axis=0,
        concat_axis=0,
        tiled=True,
    )
    delta_rows = (
        jnp.zeros((row_count + 1, feat_width), jnp.bfloat16)
        .at[routes]
        .set(returned.reshape(slot_total, feat_width))[:row_count]
    )
    col_start = lax.axis_index("tensor") * feat_width
    partial_value = jnp.dot(tokens, proj, preferred_element_type=jnp.float32)
    own_cols = lax.dynamic_slice_in_dim(
        partial_value, col_start, feat_width, 1
    ) + delta_rows.astype(jnp.float32)
    partial_value = lax.dynamic_update_slice_in_dim(partial_value, own_cols, col_start, 1)
    hidden = lax.psum_scatter(
        partial_value.astype(jnp.bfloat16), "tensor", scatter_dimension=1, tiled=True
    ).astype(jnp.float32)
    square_total = lax.psum(jnp.sum(hidden * hidden, axis=1), "tensor")
    inv_rms = lax.rsqrt(square_total / MODEL_WIDTH + 1e-05)[:, None]
    scaled = hidden * inv_rms
    gain_row = gain[None, :]
    normed = scaled * gain_row
    draft = normed.astype(jnp.bfloat16)
    weighted = gain_row * ((normed - target.astype(jnp.float32)) / 8.0)
    grad_total = lax.psum(jnp.sum(weighted * scaled, axis=1), "tensor")
    grad_hidden = (inv_rms * (weighted - scaled * (grad_total / MODEL_WIDTH)[:, None])).astype(
        jnp.bfloat16
    )
    grad_send = to_padded(grad_hidden, routes).reshape(dp_count, slot_cap, feat_width)
    grad_arrived = lax.all_to_all(grad_send, "dp", split_axis=0, concat_axis=0, tiled=True)
    grad_padded = to_padded(grad_arrived.reshape(slot_total, feat_width), positions).reshape(
        block_count, block_rows, feat_width
    )
    onehot = (
        local_tenant_index[:, None]
        == jnp.arange(adapter_down_weight.shape[0], dtype=jnp.int32)[None, :]
    ).astype(jnp.float32)
    up_part = 2.0 * jnp.einsum(
        "brp,bpo->bro", rank_act, grad_padded, preferred_element_type=jnp.float32
    )
    grad_up = jnp.einsum("bt,bro->tro", onehot, up_part, precision=lax.Precision.HIGHEST).astype(
        jnp.bfloat16
    )
    back_part = 2.0 * jnp.einsum(
        "bpo,bro->brp", grad_padded, up_weight_tiles, preferred_element_type=jnp.float32
    )
    back_act = lax.psum(back_part.astype(jnp.bfloat16), "tensor")
    down_part = jnp.einsum(
        "brp,bpk->brk", back_act, feat_padded, preferred_element_type=jnp.float32
    )
    grad_down = jnp.einsum(
        "bt,brk->trk", onehot, down_part, precision=lax.Precision.HIGHEST
    ).astype(jnp.bfloat16)
    return (draft, grad_down, grad_up)


def solution(mesh):
    return jax.shard_map(
        body,
        mesh=mesh,
        in_specs=(
            P("dp", "tensor"),
            P("tensor", None),
            P("tensor"),
            P("dp", "tensor"),
            P("dp", None, "tensor"),
            P("dp", None, "tensor"),
            P("dp", None, None),
            P("dp", None),
            P("dp", None),
        ),
        out_specs=(P("dp", "tensor"), P("dp", None, "tensor"), P("dp", None, "tensor")),
        check_vma=False,
    )
```

profile of v0, /device:TPU:4, one launch (start us, length us, event | category | flops | bytes accessed | tf_op | source)
XLA Modules:
  0.0 718.3 jit_solution(15485561268796979615)
XLA Ops:
  9.2 5.4 gather_fusion.1
  14.6 7.6 %all-to-all-start = ((bf16[16,96,512]{2,1,0:T(8,128)(2,1)}), bf16[16,96,512]{2,1,0:T(8,128)(2,1)S(1)}, u32[]{:S(2)}, u32[]{:S(2)}) async-start(bf16[16,96,512]{2,1,0:T(8,128)(2,1)} %bitcast.3), calls=%async_computation | async-start | bytes 3145728 | tf_op jit(solution)/shard_map/all_to_all | solution.py:35
  24.3 18.4 %all-to-all-done = bf16[16,96,512]{2,1,0:T(8,128)(2,1)S(1)} async-done(((bf16[16,96,512]{2,1,0:T(8,128)(2,1)}), bf16[16,96,512]{2,1,0:T(8,128)(2,1)S(1)}, u32[]{:S(2)}, u32[]{:S(2)}) %all-to-all-start) | async-done | bytes 1572896 | tf_op jit(solution)/shard_map/all_to_all | solution.py:35
  45.4 11.0 %gather_fusion.2 = bf16[3584,512]{1,0:T(8,128)(2,1)} fusion(bf16[1537,512]{1,0:T(8,128)(2,1)S(1)} %concatenate.13, s32[4096]{0:T(1024)S(1)} %pad_clamp_fusion), kind=kCustom, calls=%fused_computation.2 | custom fusion | bytes 7354368 | tf_op jit(solution)/shard_map/gather | solution.py:11
  56.4 4.8 convolution_convert_fusion
  61.9 137.7 %all-reduce.7.cloned.1.call-done = bf16[28,64,128]{2,1,0:T(8,128)(2,1)} async-done(((bf16[28,64,128]{2,1,0:T(8,128)(2,1)}), bf16[28,64,128]{2,1,0:T(8,128)(2,1)}) %all-reduce.7.cloned.1.call-update) | async-done | bytes 458768 | tf_op jit(solution)/shard_map/psum | solution.py:44
  199.7 4.0 multiply_convert_fusion
  203.7 17.7 %scatter_custom_fusion = bf16[1537,512]{1,0:T(8,128)(2,1)} fusion(s32[3584]{0:T(1024)S(1)} %fusion.24, bf16[3584,512]{1,0:T(8,128)(2,1)} %bitcast.40, bf16[]{:T(256)} %constant.17.clone.1), kind=kCustom, calls=%fused_computation.33 | custom fusion | bytes 1574400 | tf_op jit(solution)/shard_map/scatter | solution.py:52
  224.1 7.2 %all-to-all-start.1 = ((bf16[16,96,512]{2,1,0:T(8,128)(2,1)}), bf16[16,96,512]{2,1,0:T(8,128)(2,1)S(1)}, u32[]{:S(2)}, u32[]{:S(2)}) async-start(bf16[16,96,512]{2,1,0:T(8,128)(2,1)} %bitcast.36), calls=%async_computation.1 | async-start | bytes 3145728 | tf_op jit(solution)/shard_map/all_to_all | solution.py:54
  231.5 11.5 %fusion.33 = f32[512,8192]{1,0:T(8,128)} fusion(bf16[512,512]{1,0:T(8,128)(2,1)S(1)} %copy-done.4, bf16[512,8192]{1,0:T(8,128)(2,1)} %param.10), kind=kOutput, calls=%fused_computation.54 | convolution fusion | flops 4294967296 | bytes 25690112 | tf_op jit(solution)/shard_map/dot_general | solution.py:67
  243.0 8.8 %all-to-all-done.1 = bf16[16,96,512]{2,1,0:T(8,128)(2,1)S(1)} async-done(((bf16[16,96,512]{2,1,0:T(8,128)(2,1)}), bf16[16,96,512]{2,1,0:T(8,128)(2,1)S(1)}, u32[]{:S(2)}, u32[]{:S(2)}) %all-to-all-start.1) | async-done | bytes 1572896 | tf_op jit(solution)/shard_map/all_to_all | solution.py:54
  251.8 7.3 %scatter_custom_fusion.1 = bf16[513,512]{1,0:T(8,128)(2,1)S(1)} fusion(s32[1536]{0:T(1024)S(1)} %fusion.28, bf16[1536,512]{1,0:T(8,128)(2,1)S(1)} %bitcast.41, bf16[]{:T(256)} %constant.17.clone.1), kind=kCustom, calls=%fused_computation.35 | custom fusion | bytes 525314 | tf_op jit(solution)/shard_map/scatter | solution.py:64
  261.5 8.9 %convert_element_type.37 = bf16[512,8192]{1,0:T(8,128)(2,1)} convert(f32[512,8192]{1,0:T(8,128)} %add_dynamic-update-slice_fusion) | non-fusion elementwise | flops 4194304 | bytes 25165824 | tf_op jit(solution)/shard_map/convert_element_type | solution.py:73
  271.1 180.4 %reduce-scatter.2.cloned.1.call-done = bf16[512,512]{1,0:T(8,128)(2,1)} async-done(((bf16[512,8192]{1,0:T(8,128)(2,1)}), bf16[512,512]{1,0:T(8,128)(2,1)}) %reduce-scatter.2.cloned.1.call-update) | async-done | bytes 524304 | tf_op jit(solution)/shard_map/reduce_scatter | solution.py:72
  452.8 33.3 %psum.29 = f32[512]{0:T(512)S(1)} all-reduce(f32[512]{0:T(512)S(1)} %fusion.19), channel_id=1, replica_groups=mesh['dp'=16,'tensor'=16] {'tensor'}, use_global_device_ids=true, to_apply=%region_5.0 | all-reduce | flops 512 | bytes 4096 | tf_op jit(solution)/shard_map/psum | solution.py:75
  487.5 30.6 %psum.30 = f32[512]{0:T(512)S(1)} all-reduce(f32[512]{0:T(512)S(1)} %fusion.15), channel_id=1, replica_groups=mesh['dp'=16,'tensor'=16] {'tensor'}, use_global_device_ids=true, to_apply=%region_7.0 | all-reduce | flops 512 | bytes 4096 | tf_op jit(solution)/shard_map/psum | solution.py:82
  520.4 4.8 gather_fusion.4
  525.2 27.1 %all_to_all.15 = bf16[16,96,512]{2,1,0:T(8,128)(2,1)S(1)} all-to-all(bf16[16,96,512]{2,1,0:T(8,128)(2,1)S(1)} %bitcast.37), channel_id=1, replica_groups=mesh['dp'=16,'tensor'=16] {'dp'}, dimensions={0} | all-to-all | bytes 3145728 | tf_op jit(solution)/shard_map/all_to_all | solution.py:87
  552.4 11.0 %gather_fusion.5 = bf16[3584,512]{1,0:T(8,128)(2,1)} fusion(bf16[1537,512]{1,0:T(8,128)(2,1)S(1)} %concatenate.15, s32[4096]{0:T(1024)S(1)} %pad_clamp_fusion), kind=kCustom, calls=%fused_computation.5 | custom fusion | bytes 7354368 | tf_op jit(solution)/shard_map/gather | solution.py:11
  563.4 4.8 fusion.11
  570.9 3.7 fusion.7
  576.2 127.5 %all-reduce.9.cloned.1.call-done = bf16[28,64,128]{2,1,0:T(8,128)(2,1)} async-done(((bf16[28,64,128]{2,1,0:T(8,128)(2,1)}), bf16[28,64,128]{2,1,0:T(8,128)(2,1)}) %all-reduce.9.cloned.1.call-update) | async-done | bytes 458768 | tf_op jit(solution)/shard_map/psum | solution.py:104
  703.7 2.9 fusion.34
  706.6 3.6 fusion.4
  (52 shorter events, 24.2 us)
Async XLA Ops:
  7.2 15.1 %copy-start = (bf16[16,64,512]{2,1,0:T(8,128)(2,1)S(1)}, bf16[16,64,512]{2,1,0:T(8,128)(2,1)}, u32[]{:S(2)}) copy-start(bf16[16,64,512]{2,1,0:T(8,128)(2,1)} %param.13) | copy-start | bytes 3145732
  9.2 13.1 %copy-start.10 = (s32[1,28]{1,0:T(1,128)S(1)}, s32[1,28]{1,0:T(1,128)}, u32[]{:S(2)}) copy-start(s32[1,28]{1,0:T(1,128)} %param.17) | copy-start | bytes 340
  14.6 9.6 %copy-start.9 = (s32[1,3584]{1,0:T(1,128)S(1)}, s32[1,3584]{1,0:T(1,128)}, u32[]{:S(2)}) copy-start(s32[1,3584]{1,0:T(1,128)} %param.16) | copy-start | bytes 43012
  14.6 28.1 %all-to-all-start = ((bf16[16,96,512]{2,1,0:T(8,128)(2,1)}), bf16[16,96,512]{2,1,0:T(8,128)(2,1)S(1)}, u32[]{:S(2)}, u32[]{:S(2)}) async-start(bf16[16,96,512]{2,1,0:T(8,128)(2,1)} %bitcast.3), calls=%async_computation | async-start | bytes 3145728 | tf_op jit(solution)/shard_map/all_to_all | solution.py:35
  22.2 177.5 %all-reduce.7.cloned.1.call-start = ((), (), s32[]{:S(2)}) async-start(), calls=%async_computation.4 | async-start | bytes 917504 | tf_op jit(solution)/shard_map/psum | solution.py:44
  42.8 1.1 copy-start.3
  56.4 4.8 copy-start.5
  61.9 159.5 %copy-start.2 = (bf16[28,64,512]{2,1,0:T(8,128)(2,1)}, bf16[28,64,512]{2,1,0:T(8,128)(2,1)S(1)}, u32[]{:S(2)}) copy-start(bf16[28,64,512]{2,1,0:T(8,128)(2,1)S(1)} %gather_fusion.3) | copy-start | bytes 5505028
  203.7 27.8 %copy-start.4 = (bf16[512,512]{1,0:T(8,128)(2,1)S(1)}, bf16[512,512]{1,0:T(8,128)(2,1)}, u32[]{:S(2)}) copy-start(bf16[512,512]{1,0:T(8,128)(2,1)} %param.9) | copy-start | bytes 1572868
  224.1 27.8 %all-to-all-start.1 = ((bf16[16,96,512]{2,1,0:T(8,128)(2,1)}), bf16[16,96,512]{2,1,0:T(8,128)(2,1)S(1)}, u32[]{:S(2)}, u32[]{:S(2)}) async-start(bf16[16,96,512]{2,1,0:T(8,128)(2,1)} %bitcast.36), calls=%async_computation.1 | async-start | bytes 3145728 | tf_op jit(solution)/shard_map/all_to_all | solution.py:54
  231.3 220.3 %reduce-scatter.2.cloned.1.call-start = ((), (), s32[]{:S(2)}) async-start(), calls=%async_computation.5 | async-start | bytes 8912896 | tf_op jit(solution)/shard_map/reduce_scatter | solution.py:72
  270.5 0.7 copy-start.8
  270.5 215.6 %copy-start.6 = (bf16[512,512]{1,0:T(8,128)(2,1)S(1)}, bf16[512,512]{1,0:T(8,128)(2,1)}, u32[]{:S(2)}) copy-start(bf16[512,512]{1,0:T(8,128)(2,1)} %param.12) | copy-start | bytes 1572868
  270.5 433.2 %all-reduce.9.cloned.1.call-start = ((), (), s32[]{:S(2)}) async-start(), calls=%async_computation.6 | async-start | bytes 917504 | tf_op jit(solution)/shard_map/psum | solution.py:104
  563.4 4.8 copy-start.7
  703.7 8.1 %copy-start.1 = (bf16[16,64,512]{2,1,0:T(8,128)(2,1)S(1)}, bf16[16,64,512]{2,1,0:T(8,128)(2,1)}, u32[]{:S(2)}) copy-start(bf16[16,64,512]{2,1,0:T(8,128)(2,1)} %param.13) | copy-start | bytes 3145732
Sparse Core Ops, SparseCore 0:
  61.4 138.2 all-reduce.6
  270.6 180.8 reduce-scatter.1
  568.3 135.3 all-reduce.8
where the time goes:
time: 719 us; the launch traced here: 718 us
  waiting for transfers between devices  473 us (66%)
  blocking collectives  90.9 us (13%)
  local copies, waits for them, and re-layouts  71 us (10%)
  matrix products  37.9 us (5%)
  other arithmetic  16.4 us (2%)
  starting transfers between devices  15.1 us (2%)
  between operations  13.9 us (2%)
    reduce_scatter x1, waiting for transfers between devices, body(): lax.psum_scatter(partial_value.astype(jnp.bfloat16), 'tensor', scatter_di...  180 us
    psum x1, waiting for transfers between devices, body(): rank_act = lax.psum(rank_part.astype(jnp.bfloat16), 'tensor')  138 us
    psum x1, waiting for transfers between devices, body(): back_act = lax.psum(back_part.astype(jnp.bfloat16), 'tensor')  128 us
    psum x1, blocking collectives, body(): square_total = lax.psum(jnp.sum(hidden * hidden, axis=1), 'tensor')  33.3 us
    gather x4, local copies, waits for them, and re-layouts, to_padded(): return extended[positions]  32.3 us
    psum x1, blocking collectives, body(): grad_total = lax.psum(jnp.sum(weighted * scaled, axis=1), 'tensor')  30.6 us
    all_to_all x1, blocking collectives, body(): lax.all_to_all(grad_send, 'dp', split_axis=0, concat_axis=0, tiled=True)  27.1 us
    all_to_all x1, waiting for transfers between devices, body(): lax.all_to_all(outgoing, 'dp', split_axis=0, concat_axis=0, tiled=True)  18.4 us
  transfers between devices with their start and end apart: 5, of which 5 were waited for; matrix products, arithmetic and copies ran while one was open for 3% of the time, Pallas kernels for 0%

commit v1 on v0

v1 whole, which is shorter than its diff:
```python
import functools

import jax
import jax.numpy as jnp
from jax import lax
from jax.experimental import pallas as pl
from jax.experimental.pallas import tpu as pltpu
from jax.sharding import PartitionSpec as P

MODEL_WIDTH = 8192
MESH = pl.DeviceIdType.MESH
BF = jnp.bfloat16
F32 = jnp.float32
NT = (((1,), (1,)), ((), ()))

N_DP = 16
N_TEN = 16
NZ = 8
CAP = 96
SLOTS = N_DP * CAP
TEN = 16
RANK = 64
ROWS = 512
FEAT = 512
LANES = SLOTS // 4


def aligned(value, multiple):
    return pl.multiple_of(value, multiple)


def kernel(
    tok, proj, gain, target, down, up, rcol, rrow, tcol, trow,
    draft, gdown, gup,
    proj_v, onehot, out_slots, feat, back_slots, gslots, expand, expand_t,
    first, ring, ysend, yrecv, hidden, delta_rows, grad_rows,
    rank_part, rank_land, rank_full, back_part, back_land, back_full,
    stat_send, stat_land,
    proj_sem, a2a_sem, ring_sem, ar_sem, y_sem, stat_sem,
):
    dp = lax.axis_index("dp")
    ten = lax.axis_index("tensor")
    z, y = ten // 2, ten % 2

    barrier = pltpu.get_barrier_semaphore()

    def greet(d, carry):
        pl.semaphore_signal(
            barrier, inc=1, device_id=((dp + d) % N_DP, ten), device_id_type=MESH
        )
        pl.semaphore_signal(
            barrier, inc=1, device_id=(dp, (ten + d) % N_TEN), device_id_type=MESH
        )
        return carry

    lax.fori_loop(1, N_DP, greet, 0)

    def chunk_cols(c):
        return pl.ds(aligned(c * 1024, 1024), 1024)

    def load_proj(c):
        return pltpu.make_async_copy(
            proj.at[:, chunk_cols(c)], proj_v.at[:, chunk_cols(c)], proj_sem.at[c]
        )

    for place in (7, 1, 6, 2, 5, 3, 4, 0):
        load_proj((z + place) % NZ).start()

    for b in range(4):
        rows = pl.ds(b * 384, 384)
        hit = rcol[rows, :] == lax.broadcasted_iota(jnp.int32, (384, ROWS), 1)
        onehot[rows, :] = jnp.where(hit, 1.0, 0.0).astype(BF)

    def to_slots(src):
        def one(b, carry):
            rows = pl.ds(aligned(b * 384, 384), 384)
            out_slots[rows, :] = jnp.dot(
                onehot[rows, :], src[...], preferred_element_type=F32
            ).astype(BF)
            return carry

        lax.fori_loop(0, 4, one, 0)

    def slot_rows(s):
        return pl.ds(aligned(s * CAP, 32), CAP)

    def a2a_copy(src, dst, which, d):
        peer = (dp + d) % N_DP
        return pltpu.make_async_remote_copy(
            src_ref=src.at[slot_rows(peer), :],
            dst_ref=dst.at[slot_rows(dp), :],
            send_sem=a2a_sem.at[which, 0, d - 1],
            recv_sem=a2a_sem.at[which, 1, d - 1],
            device_id=(peer, ten),
            device_id_type=MESH,
        )

    def a2a_start(src, dst, which):
        def one(d, carry):
            a2a_copy(src, dst, which, d).start()
            return carry

        lax.fori_loop(1, N_DP, one, 0)
        dst[slot_rows(dp), :] = src[slot_rows(dp), :]

    def a2a_wait(src, dst, which):
        def one(d, carry):
            a2a_copy(src, dst, which, d).wait()
            return carry

        lax.fori_loop(1, N_DP, one, 0)

    to_slots(tok)
    pl.semaphore_wait(barrier, 2 * (N_DP - 1))
    a2a_start(out_slots, feat, 0)

    def stream_rows(i):
        return pl.ds(aligned(i * 128, 128), 128)

    def sign(i):
        return 1 - 2 * (i % 2)

    def ring_copy(s, i):
        src = first.at[i] if s == 0 else ring.at[s - 1, i]
        peer = ((z + sign(i) + NZ) % NZ) * 2 + y
        return pltpu.make_async_remote_copy(
            src_ref=src,
            dst_ref=ring.at[s, i],
            send_sem=ring_sem.at[0, s, i],
            recv_sem=ring_sem.at[1, s, i],
            device_id=(dp, peer),
            device_id_type=MESH,
        )

    def partial_tile(i, c, j):
        cols = pl.ds(aligned(c * 1024 + j * 512, 512), 512)
        return jnp.dot(
            tok[stream_rows(i), :], proj_v[:, cols], preferred_element_type=F32
        )

    def tile(j):
        return pl.ds(aligned(j * 512, 512), 512)

    def ring_step(s):
        if s == 0:
            load_proj((z + 7) % NZ).wait()
            load_proj((z + 1) % NZ).wait()
        elif s < 3:
            load_proj((z + 7 - s) % NZ).wait()
            load_proj((z + 1 + s) % NZ).wait()
        elif s == 3:
            load_proj((z + 4) % NZ).wait()

        def one(i, carry):
            c = (z + 2 * NZ - sign(i) * (s + 1)) % NZ
            if s:
                ring_copy(s - 1, i).wait_recv()

            def cols(j, carry):
                part = partial_tile(i, c, j)
                if s == 0:
                    first[i, :, tile(j)] = part.astype(BF)
                else:
                    ring[s - 1, i, :, tile(j)] = (
                        part + ring[s - 1, i, :, tile(j)].astype(F32)
                    ).astype(BF)
                return carry

            lax.fori_loop(0, 2, cols, 0)
            ring_copy(s, i).start()
            return carry

        lax.fori_loop(0, 4, one, 0)

    def chunk(arr, t):
        return arr.at[
            pl.ds(aligned((t // 4) * 16, 16), 16), pl.ds(aligned((t % 4) * LANES, 128), LANES)
        ]

    def scatter_copy(part, land, which, d):
        peer = (ten + d) % N_TEN
        return pltpu.make_async_remote_copy(
            src_ref=chunk(part, peer),
            dst_ref=land.at[d - 1],
            send_sem=ar_sem.at[which, 0, d - 1],
            recv_sem=ar_sem.at[which, 1, d - 1],
            device_id=(dp, peer),
            device_id_type=MESH,
        )

    def spread_copy(full, which, d):
        return pltpu.make_async_remote_copy(
            src_ref=chunk(full, ten),
            dst_ref=chunk(full, ten),
            send_sem=ar_sem.at[which, 2, d - 1],
            recv_sem=ar_sem.at[which, 3, d - 1],
            device_id=(dp, (ten + d) % N_TEN),
            device_id_type=MESH,
        )

    def each_peer(action):
        def one(d, carry):
            action(d)
            return carry

        lax.fori_loop(1, N_TEN, one, 0)

    def ar_first(part, land, which):
        each_peer(lambda d: scatter_copy(part, land, which, d).start())

    def ar_second(part, land, full, which):
        each_peer(lambda d: scatter_copy(part, land, which, d).wait())
        total = chunk(part, ten)[...].astype(F32)
        for d in range(N_TEN - 1):
            total = total + land[d].astype(F32)
        chunk(full, ten)[...] = total.astype(BF)
        each_peer(lambda d: spread_copy(full, which, d).start())

    def ar_wait(full, which):
        each_peer(lambda d: spread_copy(full, which, d).wait())

    def low_rank(weights, rows_ref, scale, out):
        def one(j, carry):
            lanes = pl.ds(aligned(j * 256, 256), 256)
            full = lax.dot_general(
                weights[...], rows_ref[lanes, :], NT, preferred_element_type=F32
            )
            tenant = jnp.broadcast_to(trow[:, lanes], (RANK, 256))
            total = jnp.zeros((RANK, 256), F32)
            for t in range(TEN):
                total = total + jnp.where(
                    tenant == t, full[t * RANK : (t + 1) * RANK, :], 0.0
                )
            out[:, lanes] = (scale * total).astype(BF)
            return carry

        lax.fori_loop(0, SLOTS // 256, one, 0)

    def spread_tenants(full):
        def one(j, carry):
            lanes = pl.ds(aligned(j * 256, 256), 256)
            value = full[:, lanes].astype(F32)
            tenant = jnp.broadcast_to(trow[:, lanes], (RANK, 256))
            for t in range(TEN):
                expand_t[t * RANK : (t + 1) * RANK, lanes] = jnp.where(
                    tenant == t, value, 0.0
                ).astype(BF)
            return carry

        lax.fori_loop(0, SLOTS // 256, one, 0)

    def grouped_outer(rows_ref, scale, out):
        def one(t, carry):
            rows = pl.ds(aligned(t * 256, 256), 256)
            out[rows, :] = (
                scale
                * jnp.dot(expand_t[rows, :], rows_ref[...], preferred_element_type=F32)
            ).astype(BF)
            return carry

        lax.fori_loop(0, TEN * RANK // 256, one, 0)

    ring_step(0)
    ring_step(1)

    a2a_wait(out_slots, feat, 0)
    low_rank(down, feat, 1.0, rank_part)
    ar_first(rank_part, rank_land, 0)

    ring_step(2)

    ar_second(rank_part, rank_land, rank_full, 0)

    ring_step(3)

    ar_wait(rank_full, 0)

    def deltas(b, carry):
        rows = pl.ds(aligned(b * 256, 256), 256)
        value = rank_full[:, rows].astype(F32)
        twice = jnp.concatenate([value, value], axis=0).T
        lane = lax.broadcasted_iota(jnp.int32, (256, 128), 1)
        tenant = jnp.broadcast_to(tcol[rows, :], (256, 128)) - jnp.where(
            lane >= RANK, 1, 0
        )
        for j in range(TEN // 2):
            expand[:, j * 128 : (j + 1) * 128] = jnp.where(
                tenant == 2 * j, twice, 0.0
            ).astype(BF)
        out_slots[rows, :] = (
            2.0 * jnp.dot(expand[...], up[...], preferred_element_type=F32)
        ).astype(BF)
        return carry

    lax.fori_loop(0, SLOTS // 256, deltas, 0)
    a2a_start(out_slots, back_slots, 1)

    ring_step(4)

    spread_tenants(rank_full)

    ring_step(5)
    ring_step(6)

    a2a_wait(out_slots, back_slots, 1)

    def scatter_rows(b, carry):
        rows = pl.ds(aligned(b * 128, 128), 128)
        hit = lax.broadcasted_iota(jnp.int32, (128, SLOTS), 0) + b * 128 == (
            jnp.broadcast_to(rrow[...], (128, SLOTS))
        )
        delta_rows[rows, :] = jnp.dot(
            jnp.where(hit, 1.0, 0.0).astype(BF),
            back_slots[...],
            preferred_element_type=F32,
        )
        return carry

    lax.fori_loop(0, 4, scatter_rows, 0)

    load_proj(z).wait()

    def y_copy(i):
        return pltpu.make_async_remote_copy(
            src_ref=ysend.at[i],
            dst_ref=yrecv.at[i],
            send_sem=y_sem.at[0, i],
            recv_sem=y_sem.at[1, i],
            device_id=(dp, z * 2 + 1 - y),
            device_id_type=MESH,
        )

    def last_hop(i, carry):
        ring_copy(6, i).wait_recv()
        ysend[i] = (
            partial_tile(i, z, 1 - y) + ring[6, i, :, tile(1 - y)].astype(F32)
        ).astype(BF)
        y_copy(i).start()
        hidden[stream_rows(i), :] = (
            partial_tile(i, z, y)
            + ring[6, i, :, tile(y)].astype(F32)
            + delta_rows[stream_rows(i), :]
        )
        return carry

    lax.fori_loop(0, 4, last_hop, 0)

    def stats(i, carry):
        y_copy(i).wait()
        rows = stream_rows(i)
        h = hidden[rows, :] + yrecv[i].astype(F32)
        hidden[rows, :] = h
        g = gain[...]
        gh = g * h
        s1 = jnp.sum(h * h, axis=1, keepdims=True)
        s2 = jnp.sum(gh * gh, axis=1, keepdims=True)
        s3 = jnp.sum(gh * target[rows, :].astype(F32), axis=1, keepdims=True)
        lane = lax.broadcasted_iota(jnp.int32, (128, 128), 1)
        table = jnp.where(lane == 0, s1, jnp.where(lane == 1, s2, s3))
        stat_send[i] = table.T[0:8, :]
        return carry

    lax.fori_loop(0, 4, stats, 0)

    def stat_copy(d):
        return pltpu.make_async_remote_copy(
            src_ref=stat_send,
            dst_ref=stat_land.at[d - 1],
            send_sem=stat_sem.at[0, d - 1],
            recv_sem=stat_sem.at[1, d - 1],
            device_id=(dp, (ten + d) % N_TEN),
            device_id_type=MESH,
        )

    each_peer(lambda d: stat_copy(d).start())
    each_peer(lambda d: stat_copy(d).wait())

    def grads(i, carry):
        total = stat_send[i]
        for d in range(N_TEN - 1):
            total = total + stat_land[d, i]
        table = jnp.concatenate([total, jnp.zeros((120, 128), F32)], axis=0).T
        rows = stream_rows(i)
        inv = lax.rsqrt(table[:, 0:1] / MODEL_WIDTH + 1e-05)
        dot = inv * (inv * table[:, 1:2] - table[:, 2:3]) / 8.0
        g = gain[...]
        scaled = hidden[rows, :] * inv
        normed = scaled * g
        draft[rows, :] = normed.astype(BF)
        weighted = g * ((normed - target[rows, :].astype(F32)) / 8.0)
        grad_rows[rows, :] = (inv * (weighted - scaled * (dot / MODEL_WIDTH))).astype(BF)
        return carry

    lax.fori_loop(0, 4, grads, 0)

    to_slots(grad_rows)
    a2a_start(out_slots, gslots, 2)
    a2a_wait(out_slots, gslots, 2)
    low_rank(up, gslots, 2.0, back_part)
    ar_first(back_part, back_land, 1)
    ar_second(back_part, back_land, back_full, 1)
    grouped_outer(gslots, 2.0, gup)
    ar_wait(back_full, 1)
    spread_tenants(back_full)
    grouped_outer(feat, 1.0, gdown)

    for s in range(NZ - 1):

        def drain(i, carry, s=s):
            ring_copy(s, i).wait_send()
            return carry

        lax.fori_loop(0, 4, drain, 0)


def slot_tenants(positions, block_tenant):
    tenant = jnp.repeat(block_tenant, positions.shape[0] // block_tenant.shape[0]) + 1
    high = positions[None, :] // 64 == jnp.arange(SLOTS // 64, dtype=jnp.int32)[:, None]
    low = positions[:, None] % 64 == jnp.arange(64, dtype=jnp.int32)[None, :]
    table = jnp.dot(
        high.astype(BF),
        jnp.where(low, tenant[:, None], 0).astype(BF),
        preferred_element_type=F32,
    )
    return table.reshape(SLOTS).astype(jnp.int32) - 1


def body(
    tokens,
    proj,
    gain,
    target,
    adapter_down_weight,
    adapter_up_weight,
    source_row_index,
    padded_row_index,
    padded_block_tenant,
):
    routes = source_row_index[0].reshape(SLOTS)
    tenants = slot_tenants(padded_row_index[0], padded_block_tenant[0])
    vmem = pl.BlockSpec(memory_space=pltpu.VMEM)
    wide = TEN * RANK
    draft, grad_down, grad_up = pl.pallas_call(
        kernel,
        out_shape=(
            jax.ShapeDtypeStruct((ROWS, FEAT), BF),
            jax.ShapeDtypeStruct((wide, FEAT), BF),
            jax.ShapeDtypeStruct((wide, FEAT), BF),
        ),
        in_specs=[vmem, pl.BlockSpec(memory_space=pl.ANY)] + [vmem] * 8,
        out_specs=(vmem, vmem, vmem),
        scratch_shapes=[
            pltpu.VMEM((FEAT, MODEL_WIDTH), BF),
            pltpu.VMEM((SLOTS, ROWS), BF),
            pltpu.VMEM((SLOTS, FEAT), BF),
            pltpu.VMEM((SLOTS, FEAT), BF),
            pltpu.VMEM((SLOTS, FEAT), BF),
            pltpu.VMEM((SLOTS, FEAT), BF),
            pltpu.VMEM((256, wide), BF),
            pltpu.VMEM((wide, SLOTS), BF),
            pltpu.VMEM((4, 128, 1024), BF),
            pltpu.VMEM((NZ - 1, 4, 128, 1024), BF),
            pltpu.VMEM((4, 128, FEAT), BF),
            pltpu.VMEM((4, 128, FEAT), BF),
            pltpu.VMEM((ROWS, FEAT), F32),
            pltpu.VMEM((ROWS, FEAT), F32),
            pltpu.VMEM((ROWS, FEAT), BF),
            pltpu.VMEM((RANK, SLOTS), BF),
            pltpu.VMEM((N_TEN - 1, 16, LANES), BF),
            pltpu.VMEM((RANK, SLOTS), BF),
            pltpu.VMEM((RANK, SLOTS), BF),
            pltpu.VMEM((N_TEN - 1, 16, LANES), BF),
            pltpu.VMEM((RANK, SLOTS), BF),
            pltpu.VMEM((4, 8, 128), F32),
            pltpu.VMEM((N_TEN - 1, 4, 8, 128), F32),
            pltpu.SemaphoreType.DMA((NZ,)),
            pltpu.SemaphoreType.DMA((3, 2, N_DP - 1)),
            pltpu.SemaphoreType.DMA((2, NZ - 1, 4)),
            pltpu.SemaphoreType.DMA((2, 4, N_TEN - 1)),
            pltpu.SemaphoreType.DMA((2, 4)),
            pltpu.SemaphoreType.DMA((2, N_TEN - 1)),
        ],
        compiler_params=pltpu.CompilerParams(
            collective_id=0, has_side_effects=True, vmem_limit_bytes=58 << 20
        ),
        name="step",
    )(
        tokens,
        proj,
        gain.reshape(1, FEAT),
        target,
        adapter_down_weight.reshape(wide, FEAT),
        adapter_up_weight.reshape(wide, FEAT),
        routes.reshape(SLOTS, 1),
        routes.reshape(1, SLOTS),
        tenants.reshape(SLOTS, 1),
        tenants.reshape(1, SLOTS),
    )
    return (
        draft,
        grad_down.reshape(TEN, RANK, FEAT),
        grad_up.reshape(TEN, RANK, FEAT),
    )


def solution(mesh):
    return jax.shard_map(
        body,
        mesh=mesh,
        in_specs=(
            P("dp", "tensor"),
            P("tensor", None),
            P("tensor"),
            P("dp", "tensor"),
            P("dp", None, "tensor"),
            P("dp", None, "tensor"),
            P("dp", None, None),
            P("dp", None),
            P("dp", None),
        ),
        out_specs=(P("dp", "tensor"), P("dp", None, "tensor"), P("dp", None, "tensor")),
        check_vma=False,
    )
```

time: 719 us -> 183 us (0.25)
  waiting for transfers between devices: 473 us -> 0 us
  Pallas kernels: 0 us -> 166 us
  blocking collectives: 90.9 us -> 0 us
  local copies, waits for them, and re-layouts: 71 us -> 10.5 us
  matrix products: 37.9 us -> 1.13 us
  starting transfers between devices: 15.1 us -> 0 us
  other arithmetic: 16.4 us -> 1.52 us
  between operations: 13.9 us -> 0.67 us
    psum x2 -> x0, waiting for transfers between devices: 265 us -> none  [the longest x1 138 us: body(): rank_act = lax.psum(rank_part.astype(jnp.bfloat16), 'tensor')]
    reduce_scatter x1 -> x0, waiting for transfers between devices: 180 us -> none  [body(): lax.psum_scatter(partial_value.astype(jnp.bfloat16), 'tensor', scatter_di...]
    pallas_call x0 -> x1, Pallas kernels: none -> 166 us  [body(): pl.pallas_call(kernel, out_shape=(jax.ShapeDtypeStruct((ROWS, FEAT), BF),...]
    psum x2 -> x0, blocking collectives: 63.9 us -> none  [the longest x1 33.3 us: body(): square_total = lax.psum(jnp.sum(hidden * hidden, axis=1), 'tensor')]
    dot_general x8 -> x1, matrix products: 37.9 us -> 1.13 us  [slot_tenants(): jnp.dot(high.astype(BF), jnp.where(low, tenant[:, None], 0).astype(BF), p...]
    gather x6 -> x0, local copies, waits for them, and re-layouts: 34.9 us -> none  [the longest x4 32.3 us: to_padded(): return extended[positions]]
    all_to_all x2 -> x0, waiting for transfers between devices: 27.3 us -> none  [the longest x1 18.4 us: body(): lax.all_to_all(outgoing, 'dp', split_axis=0, concat_axis=0, tiled=True)]
    all_to_all x1 -> x0, blocking collectives: 27.1 us -> none  [body(): lax.all_to_all(grad_send, 'dp', split_axis=0, concat_axis=0, tiled=True)]
  transfers between devices with their start and end apart: 5 -> 0, of which waited for: 5 -> 0; matrix products, arithmetic and copies ran while one was open for 3% -> 0% of each run, Pallas kernels for 0% -> 0%
where the time goes in v1:
time: 183 us; the launch traced here: 180 us
  Pallas kernels  166 us (91%)
  local copies, waits for them, and re-layouts  10.5 us (6%)
    pallas_call x1, Pallas kernels, body(): pl.pallas_call(kernel, out_shape=(jax.ShapeDtypeStruct((ROWS, FEAT), BF),...  166 us
    unnamed x7, local copies, waits for them, and re-layouts  5.22 us

profile of v1, /device:TPU:4, one launch (start us, length us, event | category | flops | bytes accessed | tf_op | source)
XLA Modules:
  0.0 180.1 jit_solution(879207479046546942)
XLA Ops:
  0.6 0.0 copy-start.1
  0.6 0.7 add_bitcast_fusion
  1.3 1.4 reshape_reshape_squeeze.7.rrow
  2.7 0.1 broadcast_bitcast_fusion
  2.7 0.8 fusion.6
  3.6 1.1 fusion
  4.7 0.7 sub.17.trow
  5.4 1.6 sub.18.tcol
  7.0 0.0 copy-done.1
  7.0 1.6 reshape_reshape_squeeze.8.rcol
  8.6 166.3 %step.1 = (bf16[512,512]{1,0:T(8,128)(2,1)}, bf16[1024,512]{1,0:T(8,128)(2,1)}, bf16[1024,512]{1,0:T(8,128)(2,1)}) custom-call(bf16[512,512]{1,0:T(8,128)(2,1)} %tok.1, bf16[512,8192]{1,0:T(8,128)(2,1)} %proj.1, f32[1,512]{1,0:T(1,128)} %bitcast.13, bf16[512,512]{1,0:T(8,128)(2,1)} %target.1, bf16[1024,512]{1,0:T(8,128)(2,1)} %bitcast.9, ...), custom_call_target="tpu_custom_call" | custom-call | tf_op jit(solution)/shard_map/step/pallas_call | solution.py:443
  174.9 0.0 copy-start
  174.9 2.0 %copy.17 = bf16[512,512]{1,0:T(8,128)(2,1)} copy(bf16[512,512]{1,0:T(8,128)(2,1)} %get-tuple-element.14) | data formatting | bytes 1048576
  176.9 2.3 %copy.18 = bf16[16,64,512]{2,1,0:T(8,128)(2,1)} copy(bf16[16,64,512]{2,1,0:T(8,128)(2,1)} %bitcast.12) | data formatting | bytes 2097152
  179.1 0.0 copy-done
  179.2 1.0 copy.19
  (1 shorter events, 0.0 us)
Async XLA Ops:
  0.6 6.4 %copy-start.1 = (s32[1,16,96]{2,1,0:T(8,128)S(1)}, s32[1,16,96]{2,1,0:T(8,128)}, u32[]{:S(2)}) copy-start(s32[1,16,96]{2,1,0:T(8,128)} %param.15) | copy-start | bytes 18436
  174.9 4.3 %copy-start = (bf16[1024,512]{1,0:T(8,128)(2,1)S(1)}, bf16[1024,512]{1,0:T(8,128)(2,1)}, u32[]{:S(2)}) copy-start(bf16[1024,512]{1,0:T(8,128)(2,1)} %get-tuple-element.8) | copy-start | bytes 3145732

commit v2 on v1

v2 whole, which is shorter than its diff:
```python
import jax
import jax.numpy as jnp
from jax import lax
from jax.experimental import pallas as pl
from jax.experimental.pallas import tpu as pltpu
from jax.sharding import PartitionSpec as P

MODEL_WIDTH = 8192
MESH = pl.DeviceIdType.MESH
BF = jnp.bfloat16
F32 = jnp.float32
NT = (((1,), (1,)), ((), ()))
TN = (((0,), (0,)), ((), ()))

N_DP = 16
N_TEN = 16
NZ = 8
CAP = 96
SLOTS = N_DP * CAP
TEN = 16
RANK = 64
ROWS = 512
FEAT = 512
LANES = SLOTS // 4
PHASES = 2
WIDE = FEAT // PHASES


def aligned(value, multiple):
    return pl.multiple_of(value, multiple)


def kernel(
    tok, proj, gain, target, down, up, routes, positions, blocks,
    draft, gdown, gup,
    proj_v, onehot, tok_out, tgt_out, delta_out, h_out, feat, tgt_slots,
    back_slots, h_slots, gslots, expand, expand_t,
    first, ring, ysend, yrecv, hidden, delta_rows, h_rows,
    rank_part, rank_land, rank_full, back_part, back_land, back_full,
    trow, tcol, stat_send, stat_land, scal_send, scal_land,
    proj_sem, a2a_sem, h_sem, scal_sem, ring_sem, ar_sem, y_sem, stat_sem,
):
    dp = lax.axis_index("dp")
    ten = lax.axis_index("tensor")
    z, y = ten // 2, ten % 2

    barrier = pltpu.get_barrier_semaphore()

    def greet(d, carry):
        pl.semaphore_signal(
            barrier, inc=1, device_id=((dp + d) % N_DP, ten), device_id_type=MESH
        )
        pl.semaphore_signal(
            barrier, inc=1, device_id=(dp, (ten + d) % N_TEN), device_id_type=MESH
        )
        return carry

    lax.fori_loop(1, N_DP, greet, 0)

    def chunk_cols(c):
        return pl.ds(aligned(c * 1024, 1024), 1024)

    def load_proj(c):
        return pltpu.make_async_copy(
            proj.at[:, chunk_cols(c)], proj_v.at[:, chunk_cols(c)], proj_sem.at[c]
        )

    for place in (7, 1, 6, 2, 5, 3, 4, 0):
        load_proj((z + place) % NZ).start()

    route = jnp.concatenate(
        [routes[0].astype(F32), jnp.zeros((N_DP, 128 - CAP), F32)], axis=1
    )
    route = jnp.concatenate([route, jnp.zeros((128 - N_DP, 128), F32)], axis=0).T
    row_number = lax.broadcasted_iota(jnp.int32, (CAP, ROWS), 1).astype(F32)
    for d in range(N_DP):
        hit = jnp.broadcast_to(route[0:CAP, d : d + 1], (CAP, ROWS)) == row_number
        onehot[d * CAP : (d + 1) * CAP, :] = jnp.where(hit, 1.0, 0.0).astype(BF)

    def to_slots(src, dst):
        def one(b, carry):
            rows = pl.ds(aligned(b * 384, 384), 384)
            dst[rows, :] = jnp.dot(
                onehot[rows, :], src[...], preferred_element_type=F32
            ).astype(BF)
            return carry

        lax.fori_loop(0, 4, one, 0)

    def slot_rows(s):
        return pl.ds(aligned(s * CAP, 32), CAP)

    def a2a_copy(src, dst, sems, d):
        peer = (dp + d) % N_DP
        return pltpu.make_async_remote_copy(
            src_ref=src.at[slot_rows(peer), :],
            dst_ref=dst.at[slot_rows(dp), :],
            send_sem=sems.at[0, d - 1],
            recv_sem=sems.at[1, d - 1],
            device_id=(peer, ten),
            device_id_type=MESH,
        )

    def each_peer(action):
        def one(d, carry):
            action(d)
            return carry

        lax.fori_loop(1, N_TEN, one, 0)

    def a2a_start(src, dst, sems):
        each_peer(lambda d: a2a_copy(src, dst, sems, d).start())
        dst[slot_rows(dp), :] = src[slot_rows(dp), :]

    def a2a_wait(src, dst, sems):
        each_peer(lambda d: a2a_copy(src, dst, sems, d).wait())

    to_slots(tok, tok_out)
    pl.semaphore_wait(barrier, 2 * (N_DP - 1))
    a2a_start(tok_out, feat, a2a_sem.at[0])

    def stream_rows(i):
        return pl.ds(aligned(i * 128, 128), 128)

    def sign(i):
        return 1 - 2 * (i % 2)

    def ring_copy(p, s, i):
        src = first.at[p, i] if s == 0 else ring.at[p, s - 1, i]
        peer = ((z + sign(i) + NZ) % NZ) * 2 + y
        return pltpu.make_async_remote_copy(
            src_ref=src,
            dst_ref=ring.at[p, s, i],
            send_sem=ring_sem.at[0, p, s, i],
            recv_sem=ring_sem.at[1, p, s, i],
            device_id=(dp, peer),
            device_id_type=MESH,
        )

    def partial_tile(p, i, c, j):
        cols = pl.ds(aligned(c * 1024 + j * 512 + p * WIDE, 128), WIDE)
        return jnp.dot(
            tok[stream_rows(i), :], proj_v[:, cols], preferred_element_type=F32
        )

    def ring_step(p, s):
        if p == 0 and s == 0:
            load_proj((z + 7) % NZ).wait()
            load_proj((z + 1) % NZ).wait()
        elif p == 0 and s < 3:
            load_proj((z + 7 - s) % NZ).wait()
            load_proj((z + 1 + s) % NZ).wait()
        elif p == 0 and s == 3:
            load_proj((z + 4) % NZ).wait()

        def one(i, carry):
            c = (z + 2 * NZ - sign(i) * (s + 1)) % NZ
            if s:
                ring_copy(p, s - 1, i).wait_recv()
            for j in range(2):
                part = partial_tile(p, i, c, j)
                cols = pl.ds(j * WIDE, WIDE)
                if s == 0:
                    first[p, i, :, cols] = part.astype(BF)
                else:
                    ring[p, s - 1, i, :, cols] = (
                        part + ring[p, s - 1, i, :, cols].astype(F32)
                    ).astype(BF)
            ring_copy(p, s, i).start()
            return carry

        lax.fori_loop(0, 4, one, 0)

    def y_copy(p, i):
        return pltpu.make_async_remote_copy(
            src_ref=ysend.at[p, i],
            dst_ref=yrecv.at[p, i],
            send_sem=y_sem.at[0, p, i],
            recv_sem=y_sem.at[1, p, i],
            device_id=(dp, z * 2 + 1 - y),
            device_id_type=MESH,
        )

    def half(j):
        return pl.ds(aligned(j * WIDE, 128), WIDE)

    def last_hop(p):
        if p == 0:
            load_proj(z).wait()

        def one(i, carry):
            ring_copy(p, NZ - 2, i).wait_recv()
            ysend[p, i] = (
                partial_tile(p, i, z, 1 - y)
                + ring[p, NZ - 2, i, :, half(1 - y)].astype(F32)
            ).astype(BF)
            y_copy(p, i).start()
            hidden[p, stream_rows(i), :] = partial_tile(p, i, z, y) + ring[
                p, NZ - 2, i, :, half(y)
            ].astype(F32)
            return carry

        lax.fori_loop(0, 4, one, 0)

    def finish(p):
        def one(i, carry):
            y_copy(p, i).wait()
            rows = stream_rows(i)
            total = hidden[p, rows, :] + yrecv[p, i].astype(F32)
            hidden[p, rows, :] = total
            h_rows[rows, :] = total.astype(BF)
            return carry

        lax.fori_loop(0, 4, one, 0)
        to_slots(h_rows, h_out.at[p])
        a2a_start(h_out.at[p], h_slots.at[p], h_sem.at[p])

    def chunk(arr, t):
        return arr.at[
            pl.ds(aligned((t // 4) * 16, 16), 16), pl.ds(aligned((t % 4) * LANES, 128), LANES)
        ]

    def scatter_copy(part, land, which, d):
        peer = (ten + d) % N_TEN
        return pltpu.make_async_remote_copy(
            src_ref=chunk(part, peer),
            dst_ref=land.at[d - 1],
            send_sem=ar_sem.at[which, 0, d - 1],
            recv_sem=ar_sem.at[which, 1, d - 1],
            device_id=(dp, peer),
            device_id_type=MESH,
        )

    def spread_copy(full, which, d):
        return pltpu.make_async_remote_copy(
            src_ref=chunk(full, ten),
            dst_ref=chunk(full, ten),
            send_sem=ar_sem.at[which, 2, d - 1],
            recv_sem=ar_sem.at[which, 3, d - 1],
            device_id=(dp, (ten + d) % N_TEN),
            device_id_type=MESH,
        )

    def ar_first(part, land, which):
        each_peer(lambda d: scatter_copy(part, land, which, d).start())

    def ar_second(part, land, full, which):
        each_peer(lambda d: scatter_copy(part, land, which, d).wait())
        total = chunk(part, ten)[...].astype(F32)
        for d in range(N_TEN - 1):
            total = total + land[d].astype(F32)
        chunk(full, ten)[...] = total.astype(BF)
        each_peer(lambda d: spread_copy(full, which, d).start())

    def ar_wait(full, which):
        each_peer(lambda d: spread_copy(full, which, d).wait())

    def low_rank(weights, rows_ref, scale, out):
        def one(j, carry):
            lanes = pl.ds(aligned(j * 256, 256), 256)
            full = lax.dot_general(
                weights[...], rows_ref[lanes, :], NT, preferred_element_type=F32
            )
            tenant = jnp.broadcast_to(trow[:, lanes], (RANK, 256))
            total = jnp.zeros((RANK, 256), F32)
            for t in range(TEN):
                total = total + jnp.where(
                    tenant == t + 1.0, full[t * RANK : (t + 1) * RANK, :], 0.0
                )
            out[:, lanes] = (scale * total).astype(BF)
            return carry

        lax.fori_loop(0, SLOTS // 256, one, 0)

    def spread_tenants(full):
        def one(j, carry):
            lanes = pl.ds(aligned(j * 256, 256), 256)
            value = full[:, lanes].astype(F32)
            tenant = jnp.broadcast_to(trow[:, lanes], (RANK, 256))
            for t in range(TEN):
                expand_t[t * RANK : (t + 1) * RANK, lanes] = jnp.where(
                    tenant == t + 1.0, value, 0.0
                ).astype(BF)
            return carry

        lax.fori_loop(0, SLOTS // 256, one, 0)

    def grouped_outer(rows_ref, scale, out):
        def one(t, carry):
            rows = pl.ds(aligned(t * 256, 256), 256)
            out[rows, :] = (
                scale
                * jnp.dot(expand_t[rows, :], rows_ref[...], preferred_element_type=F32)
            ).astype(BF)
            return carry

        lax.fori_loop(0, TEN * RANK // 256, one, 0)

    def slot_tenants():
        held = positions[...]
        count = held.shape[1]
        owner = jnp.concatenate(
            [
                jnp.broadcast_to(blocks[:, b : b + 1].astype(F32) + 1.0, (1, 128))
                for b in range(count // 128)
            ],
            axis=1,
        )
        high = jnp.where(
            jnp.broadcast_to(held // 128, (16, count))
            == lax.broadcasted_iota(jnp.int32, (16, count), 0),
            1.0,
            0.0,
        ).astype(BF)
        low = jnp.where(
            jnp.broadcast_to(held % 128, (128, count))
            == lax.broadcasted_iota(jnp.int32, (128, count), 0),
            jnp.broadcast_to(owner, (128, count)),
            0.0,
        ).astype(BF)
        table = lax.dot_general(high, low, NT, preferred_element_type=F32)
        columns = jnp.concatenate([table, jnp.zeros((112, 128), F32)], axis=0).T
        for a in range(SLOTS // 128):
            trow[:, a * 128 : (a + 1) * 128] = table[a : a + 1, :]
            tcol[a * 128 : (a + 1) * 128, :] = jnp.broadcast_to(
                columns[:, a : a + 1], (128, 128)
            )

    def deltas(b, carry):
        rows = pl.ds(aligned(b * 256, 256), 256)
        value = rank_full[:, rows].astype(F32)
        twice = jnp.concatenate([value, value], axis=0).T
        lane = lax.broadcasted_iota(jnp.int32, (256, 128), 1)
        tenant = tcol[rows, :] - jnp.where(lane >= RANK, 1.0, 0.0)
        for j in range(TEN // 2):
            expand[:, j * 128 : (j + 1) * 128] = jnp.where(
                tenant == 2.0 * j + 1.0, twice, 0.0
            ).astype(BF)
        delta_out[rows, :] = (
            2.0 * jnp.dot(expand[...], up[...], preferred_element_type=F32)
        ).astype(BF)
        return carry

    def scatter_rows():
        for q in range(4):
            cols = pl.ds(q * 128, 128)
            delta_rows[cols, :] = lax.dot_general(
                onehot[:, cols], back_slots[...], TN, preferred_element_type=F32
            )

    ring_step(0, 0)
    slot_tenants()
    to_slots(target, tgt_out)
    ring_step(0, 1)
    ring_step(0, 2)
    ring_step(0, 3)
    a2a_wait(tok_out, feat, a2a_sem.at[0])
    low_rank(down, feat, 1.0, rank_part)
    ar_first(rank_part, rank_land, 0)
    a2a_start(tgt_out, tgt_slots, a2a_sem.at[2])
    ring_step(0, 4)
    ring_step(0, 5)
    ar_second(rank_part, rank_land, rank_full, 0)
    ring_step(0, 6)
    ring_step(1, 0)
    last_hop(0)
    ring_step(1, 1)
    ar_wait(rank_full, 0)
    lax.fori_loop(0, SLOTS // 256, deltas, 0)
    a2a_start(delta_out, back_slots, a2a_sem.at[1])
    ring_step(1, 2)
    finish(0)
    ring_step(1, 3)
    spread_tenants(rank_full)
    ring_step(1, 4)
    ring_step(1, 5)
    ring_step(1, 6)
    a2a_wait(delta_out, back_slots, a2a_sem.at[1])
    scatter_rows()
    last_hop(1)
    finish(1)

    for i in range(4):
        rows = pl.ds(i * 128, 128)
        s1 = jnp.zeros((128, 1), F32)
        s2 = jnp.zeros((128, 1), F32)
        s3 = jnp.zeros((128, 1), F32)
        for p in range(PHASES):
            cols = pl.ds(p * WIDE, WIDE)
            h = hidden[p, rows, :] + delta_rows[rows, cols]
            hidden[p, rows, :] = h
            gh = gain[:, cols] * h
            s1 += jnp.sum(h * h, axis=1, keepdims=True)
            s2 += jnp.sum(gh * gh, axis=1, keepdims=True)
            s3 += jnp.sum(gh * target[rows, cols].astype(F32), axis=1, keepdims=True)
        lane = lax.broadcasted_iota(jnp.int32, (128, 128), 1)
        table = jnp.where(lane == 0, s1, jnp.where(lane == 1, s2, s3))
        stat_send[4 * i : 4 * i + 4, :] = table.T[0:4, :]

    def stat_copy(d):
        return pltpu.make_async_remote_copy(
            src_ref=stat_send,
            dst_ref=stat_land.at[d - 1],
            send_sem=stat_sem.at[0, d - 1],
            recv_sem=stat_sem.at[1, d - 1],
            device_id=(dp, (ten + d) % N_TEN),
            device_id_type=MESH,
        )

    each_peer(lambda d: stat_copy(d).start())
    each_peer(lambda d: stat_copy(d).wait())

    total = stat_send[...]
    for d in range(N_TEN - 1):
        total = total + stat_land[d]
    invs, dots = [], []
    for i in range(4):
        s1, s2, s3 = (total[4 * i + q : 4 * i + q + 1, :] for q in range(3))
        inv = lax.rsqrt(s1 / MODEL_WIDTH + 1e-05)
        invs.append(inv)
        dots.append(inv * (inv * s2 - s3) / (8.0 * MODEL_WIDTH))
    scalars = jnp.concatenate(
        [
            jnp.concatenate(invs, axis=1),
            jnp.concatenate(dots, axis=1),
            jnp.zeros((6, ROWS), F32),
        ],
        axis=0,
    )

    for d in range(N_DP):
        scal_send[d, :, 0:CAP] = lax.dot_general(
            scalars,
            onehot[d * CAP : (d + 1) * CAP, :].astype(F32),
            NT,
            precision=lax.Precision.HIGHEST,
            preferred_element_type=F32,
        )
        scal_send[d, :, CAP:128] = jnp.zeros((8, 128 - CAP), F32)

    def scal_copy(d):
        peer = (dp + d) % N_DP
        return pltpu.make_async_remote_copy(
            src_ref=scal_send.at[peer],
            dst_ref=scal_land.at[dp],
            send_sem=scal_sem.at[0, d - 1],
            recv_sem=scal_sem.at[1, d - 1],
            device_id=(peer, ten),
            device_id_type=MESH,
        )

    each_peer(lambda d: scal_copy(d).start())
    scal_land[dp] = scal_send[dp]

    for i in range(4):
        rows = pl.ds(i * 128, 128)
        table = jnp.concatenate([invs[i], jnp.zeros((127, 128), F32)], axis=0).T
        inv = table[:, 0:1]
        for p in range(PHASES):
            cols = pl.ds(p * WIDE, WIDE)
            draft[rows, cols] = (hidden[p, rows, :] * inv * gain[:, cols]).astype(BF)

    a2a_wait(tgt_out, tgt_slots, a2a_sem.at[2])
    for p in range(PHASES):
        a2a_wait(h_out.at[p], h_slots.at[p], h_sem.at[p])
    each_peer(lambda d: scal_copy(d).wait())

    def grads(s, carry):
        rows = slot_rows(s)
        table = jnp.concatenate([scal_land[s], jnp.zeros((120, 128), F32)], axis=0).T
        inv, dot = table[0:CAP, 0:1], table[0:CAP, 1:2]
        for p in range(PHASES):
            cols = pl.ds(p * WIDE, WIDE)
            g = gain[:, cols]
            h = h_slots[p, rows, :].astype(F32) + delta_out[rows, cols].astype(F32)
            scaled = h * inv
            weighted = g * ((scaled * g - tgt_slots[rows, cols].astype(F32)) / 8.0)
            gslots[rows, cols] = (inv * (weighted - scaled * dot)).astype(BF)
        return carry

    lax.fori_loop(0, N_DP, grads, 0)

    low_rank(up, gslots, 2.0, back_part)
    ar_first(back_part, back_land, 1)
    ar_second(back_part, back_land, back_full, 1)
    grouped_outer(gslots, 2.0, gup)
    ar_wait(back_full, 1)
    spread_tenants(back_full)
    grouped_outer(feat, 1.0, gdown)

    for p in range(PHASES):
        for s in range(NZ - 1):

            def drain(i, carry, p=p, s=s):
                ring_copy(p, s, i).wait_send()
                return carry

            lax.fori_loop(0, 4, drain, 0)


def body(
    tokens,
    proj,
    gain,
    target,
    adapter_down_weight,
    adapter_up_weight,
    source_row_index,
    padded_row_index,
    padded_block_tenant,
):
    vmem = pl.BlockSpec(memory_space=pltpu.VMEM)
    wide = TEN * RANK
    dma = pltpu.SemaphoreType.DMA
    draft, grad_down, grad_up = pl.pallas_call(
        kernel,
        out_shape=(
            jax.ShapeDtypeStruct((ROWS, FEAT), BF),
            jax.ShapeDtypeStruct((wide, FEAT), BF),
            jax.ShapeDtypeStruct((wide, FEAT), BF),
        ),
        in_specs=[vmem, pl.BlockSpec(memory_space=pl.ANY)] + [vmem] * 7,
        out_specs=(vmem, vmem, vmem),
        scratch_shapes=[
            pltpu.VMEM((FEAT, MODEL_WIDTH), BF),
            pltpu.VMEM((SLOTS, ROWS), BF),
            pltpu.VMEM((SLOTS, FEAT), BF),
            pltpu.VMEM((SLOTS, FEAT), BF),
            pltpu.VMEM((SLOTS, FEAT), BF),
            pltpu.VMEM((PHASES, SLOTS, WIDE), BF),
            pltpu.VMEM((SLOTS, FEAT), BF),
            pltpu.VMEM((SLOTS, FEAT), BF),
            pltpu.VMEM((SLOTS, FEAT), BF),
            pltpu.VMEM((PHASES, SLOTS, WIDE), BF),
            pltpu.VMEM((SLOTS, FEAT), BF),
            pltpu.VMEM((256, wide), BF),
            pltpu.VMEM((wide, SLOTS), BF),
            pltpu.VMEM((PHASES, 4, 128, 2 * WIDE), BF),
            pltpu.VMEM((PHASES, NZ - 1, 4, 128, 2 * WIDE), BF),
            pltpu.VMEM((PHASES, 4, 128, WIDE), BF),
            pltpu.VMEM((PHASES, 4, 128, WIDE), BF),
            pltpu.VMEM((PHASES, ROWS, WIDE), F32),
            pltpu.VMEM((ROWS, FEAT), F32),
            pltpu.VMEM((ROWS, WIDE), BF),
            pltpu.VMEM((RANK, SLOTS), BF),
            pltpu.VMEM((N_TEN - 1, 16, LANES), BF),
            pltpu.VMEM((RANK, SLOTS), BF),
            pltpu.VMEM((RANK, SLOTS), BF),
            pltpu.VMEM((N_TEN - 1, 16, LANES), BF),
            pltpu.VMEM((RANK, SLOTS), BF),
            pltpu.VMEM((1, SLOTS), F32),
            pltpu.VMEM((SLOTS, 128), F32),
            pltpu.VMEM((16, 128), F32),
            pltpu.VMEM((N_TEN - 1, 16, 128), F32),
            pltpu.VMEM((N_DP, 8, 128), F32),
            pltpu.VMEM((N_DP, 8, 128), F32),
            dma((NZ,)),
            dma((3, 2, N_DP - 1)),
            dma((PHASES, 2, N_DP - 1)),
            dma((2, N_DP - 1)),
            dma((2, PHASES, NZ - 1, 4)),
            dma((2, 4, N_TEN - 1)),
            dma((2, PHASES, 4)),
            dma((2, N_TEN - 1)),
        ],
        compiler_params=pltpu.CompilerParams(
            collective_id=0, has_side_effects=True, vmem_limit_bytes=58 << 20
        ),
        name="step",
    )(
        tokens,
        proj,
        gain.reshape(1, FEAT),
        target,
        adapter_down_weight.reshape(wide, FEAT),
        adapter_up_weight.reshape(wide, FEAT),
        source_row_index,
        padded_row_index,
        padded_block_tenant,
    )
    return (
        draft,
        grad_down.reshape(TEN, RANK, FEAT),
        grad_up.reshape(TEN, RANK, FEAT),
    )


def solution(mesh):
    return jax.shard_map(
        body,
        mesh=mesh,
        in_specs=(
            P("dp", "tensor"),
            P("tensor", None),
            P("tensor"),
            P("dp", "tensor"),
            P("dp", None, "tensor"),
            P("dp", None, "tensor"),
            P("dp", None, None),
            P("dp", None),
            P("dp", None),
        ),
        out_specs=(P("dp", "tensor"), P("dp", None, "tensor"), P("dp", None, "tensor")),
        check_vma=False,
    )
```

time: 183 us -> 171 us (0.934); the launches traced: 180 us -> 171 us
  local copies, waits for them, and re-layouts: 10.5 us -> 6.44 us
  Pallas kernels: 166 us -> 163 us
    another operation x2 -> x0, local copies, waits for them, and re-layouts: 2.92 us -> none  [the longest x1 1.55 us: body(): routes.reshape(SLOTS, 1)]
    pallas_call x1, Pallas kernels: 166 us -> 163 us  [body(): pl.pallas_call(kernel, out_shape=(jax.ShapeDtypeStruct((ROWS, FEAT), BF),...]
    sub x2 -> x0, local copies, waits for them, and re-layouts: 2.3 us -> none  [slot_tenants(): return table.reshape(SLOTS).astype(jnp.int32) - 1]
    unnamed x7 -> x3, local copies, waits for them, and re-layouts: 5.22 us -> 6.44 us
where the time goes in v2:
time: 171 us
  Pallas kernels  163 us (95%)
  local copies, waits for them, and re-layouts  6.44 us (4%)
    pallas_call x1, Pallas kernels, body(): pl.pallas_call(kernel, out_shape=(jax.ShapeDtypeStruct((ROWS, FEAT), BF),...  163 us
    unnamed x3, local copies, waits for them, and re-layouts  6.44 us

profile of v2, /device:TPU:4, one launch (start us, length us, event | category | flops | bytes accessed | tf_op | source)
XLA Modules:
  0.0 170.6 jit_solution(11109636567632221348)
XLA Ops:
  0.6 163.5 %step.1 = (bf16[512,512]{1,0:T(8,128)(2,1)}, bf16[1024,512]{1,0:T(8,128)(2,1)}, bf16[1024,512]{1,0:T(8,128)(2,1)}) custom-call(bf16[512,512]{1,0:T(8,128)(2,1)} %tok.1, bf16[512,8192]{1,0:T(8,128)(2,1)} %proj.1, f32[1,512]{1,0:T(1,128)} %bitcast.9, bf16[512,512]{1,0:T(8,128)(2,1)} %target.1, bf16[1024,512]{1,0:T(8,128)(2,1)} %bitcast.5, ...), custom_call_target="tpu_custom_call" | custom-call | tf_op jit(solution)/shard_map/step/pallas_call | solution.py:515
  164.1 1.9 %copy.15 = bf16[512,512]{1,0:T(8,128)(2,1)} copy(bf16[512,512]{1,0:T(8,128)(2,1)} %get-tuple-element.12) | data formatting | bytes 1048576
  166.0 2.3 %copy.16 = bf16[16,64,512]{2,1,0:T(8,128)(2,1)} copy(bf16[16,64,512]{2,1,0:T(8,128)(2,1)} %bitcast.8) | data formatting | bytes 2097152
  168.3 2.3 %copy.17 = bf16[16,64,512]{2,1,0:T(8,128)(2,1)} copy(bf16[16,64,512]{2,1,0:T(8,128)(2,1)} %bitcast.7) | data formatting | bytes 2097152

commit v3 on v2

v3 whole, which is shorter than its diff:
```python
import jax
import jax.numpy as jnp
from jax import lax
from jax.experimental import pallas as pl
from jax.experimental.pallas import tpu as pltpu
from jax.sharding import PartitionSpec as P

MODEL_WIDTH = 8192
MESH = pl.DeviceIdType.MESH
BF = jnp.bfloat16
F32 = jnp.float32
NT = (((1,), (1,)), ((), ()))
TN = (((0,), (0,)), ((), ()))

N_DP = 16
N_TEN = 16
NZ = 8
CAP = 96
SLOTS = N_DP * CAP
TEN = 16
RANK = 64
ROWS = 512
FEAT = 512
LANES = SLOTS // 4
PHASES = ((0, 384), (384, 128))


def aligned(value, multiple):
    return pl.multiple_of(value, multiple)


def kernel(
    tok, proj, gain, target, down, up, routes, positions, blocks,
    draft, gdown, gup,
    proj_v, onehot, tok_out, tgt_out, delta_out, h_out, feat, tgt_slots,
    back_slots, h_slots, gslots, expand, expand_t,
    part, first, ring, ysend, yrecv, hidden, delta_rows, h_rows,
    rank_part, rank_land, rank_full, back_part, back_land, back_full,
    trow, tcol, stat_acc, stat_send, stat_land, scal_send, scal_land,
    proj_sem, a2a_sem, h_sem, scal_sem, ring_sem, ar_sem, y_sem, stat_sem,
):
    dp = lax.axis_index("dp")
    ten = lax.axis_index("tensor")
    z, y = ten // 2, ten % 2

    barrier = pltpu.get_barrier_semaphore()

    def greet(d, carry):
        pl.semaphore_signal(
            barrier, inc=1, device_id=((dp + d) % N_DP, ten), device_id_type=MESH
        )
        pl.semaphore_signal(
            barrier, inc=1, device_id=(dp, (ten + d) % N_TEN), device_id_type=MESH
        )
        return carry

    lax.fori_loop(1, N_DP, greet, 0)

    def chunk_cols(c):
        return pl.ds(aligned(c * 1024, 1024), 1024)

    def load_proj(c):
        return pltpu.make_async_copy(
            proj.at[:, chunk_cols(c)], proj_v.at[:, chunk_cols(c)], proj_sem.at[c]
        )

    for place in (7, 1, 6, 2, 5, 3, 4, 0):
        load_proj((z + place) % NZ).start()

    route = jnp.concatenate(
        [routes[0].astype(F32), jnp.zeros((N_DP, 128 - CAP), F32)], axis=1
    )
    route = jnp.concatenate([route, jnp.zeros((128 - N_DP, 128), F32)], axis=0).T
    row_number = lax.broadcasted_iota(jnp.int32, (CAP, ROWS), 1).astype(F32)
    for d in range(N_DP):
        hit = jnp.broadcast_to(route[0:CAP, d : d + 1], (CAP, ROWS)) == row_number
        onehot[d * CAP : (d + 1) * CAP, :] = jnp.where(hit, 1.0, 0.0).astype(BF)

    def to_slots(src, dst, cols=pl.ds(0, FEAT)):
        def one(b, carry):
            rows = pl.ds(aligned(b * 384, 384), 384)
            dst[rows, cols] = jnp.dot(
                onehot[rows, :], src[:, cols], preferred_element_type=F32
            ).astype(BF)
            return carry

        lax.fori_loop(0, 4, one, 0)

    def slot_rows(s):
        return pl.ds(aligned(s * CAP, 32), CAP)

    everything = pl.ds(0, FEAT)

    def a2a_copy(src, dst, sems, cols, d):
        peer = (dp + d) % N_DP
        return pltpu.make_async_remote_copy(
            src_ref=src.at[slot_rows(peer), cols],
            dst_ref=dst.at[slot_rows(dp), cols],
            send_sem=sems.at[0, d - 1],
            recv_sem=sems.at[1, d - 1],
            device_id=(peer, ten),
            device_id_type=MESH,
        )

    def each_peer(action):
        def one(d, carry):
            action(d)
            return carry

        lax.fori_loop(1, N_TEN, one, 0)

    def a2a_start(src, dst, sems, cols=everything):
        each_peer(lambda d: a2a_copy(src, dst, sems, cols, d).start())
        dst[slot_rows(dp), cols] = src[slot_rows(dp), cols]

    def a2a_wait(src, dst, sems, cols=everything):
        each_peer(lambda d: a2a_copy(src, dst, sems, cols, d).wait())

    def stream_rows(i):
        return pl.ds(aligned(i * 128, 128), 128)

    def sign(i):
        return 1 - 2 * (i // 2)

    def part_cols(p):
        return pl.ds(*PHASES[p])

    def ring_copy(p, s, i):
        here = first.at[i] if s == 0 else ring.at[s - 1, i]
        peer = ((z + sign(i) + NZ) % NZ) * 2 + y
        return pltpu.make_async_remote_copy(
            src_ref=here.at[:, :, part_cols(p)],
            dst_ref=ring.at[s, i, :, :, part_cols(p)],
            send_sem=ring_sem.at[0, p, s, i],
            recv_sem=ring_sem.at[1, p, s, i],
            device_id=(dp, peer),
            device_id_type=MESH,
        )

    def partials(p, s):
        if p == 0 and s == 0:
            load_proj((z + 7) % NZ).wait()
            load_proj((z + 1) % NZ).wait()
        elif p == 0 and s < 3:
            load_proj((z + 7 - s) % NZ).wait()
            load_proj((z + 1 + s) % NZ).wait()
        elif p == 0 and s == 3:
            load_proj((z + 4) % NZ).wait()
        elif p == 0 and s == 7:
            load_proj(z).wait()
        start, width = PHASES[p]

        def one(way, carry):
            c = (z + 2 * NZ - (1 - 2 * way) * (s + 1)) % NZ
            rows = pl.ds(aligned(way * 256, 256), 256)
            for j in range(2):
                cols = pl.ds(aligned(c * 1024 + j * 512 + start, 128), width)
                part[way, j, :, part_cols(p)] = jnp.dot(
                    tok[rows, :], proj_v[:, cols], preferred_element_type=F32
                )
            return carry

        lax.fori_loop(0, 2, one, 0)

    def my_part(p, i, j):
        rows = pl.ds(aligned((i % 2) * 128, 128), 128)
        return part[i // 2, j, rows, part_cols(p)]

    def each_stream(action):
        def one(k, carry):
            action((k % 2) * 2 + k // 2)
            return carry

        lax.fori_loop(0, 4, one, 0)

    def first_sends(p):
        def one(i):
            for j in range(2):
                first[i, j, :, part_cols(p)] = my_part(p, i, j).astype(BF)
            ring_copy(p, 0, i).start()

        each_stream(one)
        partials(p, 1)

    def ring_step(p, s):
        def one(i):
            ring_copy(p, s - 1, i).wait_recv()
            for j in range(2):
                ring[s - 1, i, j, :, part_cols(p)] = (
                    my_part(p, i, j) + ring[s - 1, i, j, :, part_cols(p)].astype(F32)
                ).astype(BF)
            ring_copy(p, s, i).start()

        each_stream(one)
        partials(p, s + 1)

    def y_copy(p, i):
        return pltpu.make_async_remote_copy(
            src_ref=ysend.at[i, :, part_cols(p)],
            dst_ref=yrecv.at[i, :, part_cols(p)],
            send_sem=y_sem.at[0, p, i],
            recv_sem=y_sem.at[1, p, i],
            device_id=(dp, z * 2 + 1 - y),
            device_id_type=MESH,
        )

    def last_hop(p):
        cols = part_cols(p)

        def one(i):
            ring_copy(p, NZ - 2, i).wait_recv()
            ysend[i, :, cols] = (
                my_part(p, i, 1 - y) + ring[NZ - 2, i, 1 - y, :, cols].astype(F32)
            ).astype(BF)
            y_copy(p, i).start()
            hidden[stream_rows(i), cols] = my_part(p, i, y) + ring[
                NZ - 2, i, y, :, cols
            ].astype(F32)

        each_stream(one)

    def y_finish(p):
        cols = part_cols(p)

        def one(i, carry):
            y_copy(p, i).wait()
            rows = stream_rows(i)
            total = hidden[rows, cols] + yrecv[i, :, cols].astype(F32)
            hidden[rows, cols] = total
            h_rows[rows, cols] = total.astype(BF)
            return carry

        lax.fori_loop(0, 4, one, 0)

    def to_owners(p):
        to_slots(h_rows, h_out, part_cols(p))
        a2a_start(h_out, h_slots, h_sem.at[p], part_cols(p))

    def chunk(arr, t, g, n):
        wide = LANES // n
        return arr.at[
            pl.ds(aligned((t // 4) * 16, 16), 16),
            pl.ds(aligned(g * 4 * wide + (t % 4) * wide, 128), wide),
        ]

    def landed(land, d, g, n):
        return land.at[d, :, pl.ds(g * (LANES // n), LANES // n)]

    def scatter_copy(part, land, g, n, d):
        peer = (ten + d) % N_TEN
        return pltpu.make_async_remote_copy(
            src_ref=chunk(part, peer, g, n),
            dst_ref=landed(land, d - 1, g, n),
            send_sem=ar_sem.at[n - 1 + g, 0, d - 1],
            recv_sem=ar_sem.at[n - 1 + g, 1, d - 1],
            device_id=(dp, peer),
            device_id_type=MESH,
        )

    def spread_copy(full, g, n, d):
        return pltpu.make_async_remote_copy(
            src_ref=chunk(full, ten, g, n),
            dst_ref=chunk(full, ten, g, n),
            send_sem=ar_sem.at[n - 1 + g, 2, d - 1],
            recv_sem=ar_sem.at[n - 1 + g, 3, d - 1],
            device_id=(dp, (ten + d) % N_TEN),
            device_id_type=MESH,
        )

    def ar_first(part, land, g, n):
        each_peer(lambda d: scatter_copy(part, land, g, n, d).start())

    def ar_second(part, land, full, g, n):
        each_peer(lambda d: scatter_copy(part, land, g, n, d).wait())
        total = chunk(part, ten, g, n)[...].astype(F32)
        for d in range(N_TEN - 1):
            total = total + landed(land, d, g, n)[...].astype(F32)
        chunk(full, ten, g, n)[...] = total.astype(BF)
        each_peer(lambda d: spread_copy(full, g, n, d).start())

    def ar_wait(full, g, n):
        each_peer(lambda d: spread_copy(full, g, n, d).wait())

    def low_rank(weights, rows_ref, scale, out, tiles=(0, SLOTS // 256)):
        def one(j, carry):
            lanes = pl.ds(aligned(j * 256, 256), 256)
            full = lax.dot_general(
                weights[...], rows_ref[lanes, :], NT, preferred_element_type=F32
            )
            tenant = jnp.broadcast_to(trow[:, lanes], (RANK, 256))
            total = jnp.zeros((RANK, 256), F32)
            for t in range(TEN):
                total = total + jnp.where(
                    tenant == t + 1.0, full[t * RANK : (t + 1) * RANK, :], 0.0
                )
            out[:, lanes] = (scale * total).astype(BF)
            return carry

        lax.fori_loop(*tiles, one, 0)

    def spread_tenants(full, tiles=(0, SLOTS // 256)):
        def one(j, carry):
            lanes = pl.ds(aligned(j * 256, 256), 256)
            value = full[:, lanes].astype(F32)
            tenant = jnp.broadcast_to(trow[:, lanes], (RANK, 256))
            for t in range(TEN):
                expand_t[t * RANK : (t + 1) * RANK, lanes] = jnp.where(
                    tenant == t + 1.0, value, 0.0
                ).astype(BF)
            return carry

        lax.fori_loop(*tiles, one, 0)

    def grouped_outer(rows_ref, scale, out):
        def one(t, carry):
            rows = pl.ds(aligned(t * 256, 256), 256)
            out[rows, :] = (
                scale
                * jnp.dot(expand_t[rows, :], rows_ref[...], preferred_element_type=F32)
            ).astype(BF)
            return carry

        lax.fori_loop(0, TEN * RANK // 256, one, 0)

    def slot_tenants():
        held = positions[...]
        count = held.shape[1]
        owner = jnp.concatenate(
            [
                jnp.broadcast_to(blocks[:, b : b + 1].astype(F32) + 1.0, (1, 128))
                for b in range(count // 128)
            ],
            axis=1,
        )
        high = jnp.where(
            jnp.broadcast_to(held // 128, (16, count))
            == lax.broadcasted_iota(jnp.int32, (16, count), 0),
            1.0,
            0.0,
        ).astype(BF)
        low = jnp.where(
            jnp.broadcast_to(held % 128, (128, count))
            == lax.broadcasted_iota(jnp.int32, (128, count), 0),
            jnp.broadcast_to(owner, (128, count)),
            0.0,
        ).astype(BF)
        table = lax.dot_general(high, low, NT, preferred_element_type=F32)
        columns = jnp.concatenate([table, jnp.zeros((112, 128), F32)], axis=0).T
        for a in range(SLOTS // 128):
            trow[:, a * 128 : (a + 1) * 128] = table[a : a + 1, :]
            tcol[a * 128 : (a + 1) * 128, :] = jnp.broadcast_to(
                columns[:, a : a + 1], (128, 128)
            )

    def deltas(b, carry):
        rows = pl.ds(aligned(b * 256, 256), 256)
        value = rank_full[:, rows].astype(F32)
        twice = jnp.concatenate([value, value], axis=0).T
        lane = lax.broadcasted_iota(jnp.int32, (256, 128), 1)
        tenant = tcol[rows, :] - jnp.where(lane >= RANK, 1.0, 0.0)
        for j in range(TEN // 2):
            expand[:, j * 128 : (j + 1) * 128] = jnp.where(
                tenant == 2.0 * j + 1.0, twice, 0.0
            ).astype(BF)
        delta_out[rows, :] = (
            2.0 * jnp.dot(expand[...], up[...], preferred_element_type=F32)
        ).astype(BF)
        return carry

    def scatter_rows():
        for q in range(4):
            cols = pl.ds(q * 128, 128)
            delta_rows[cols, :] = lax.dot_general(
                onehot[:, cols], back_slots[...], TN, preferred_element_type=F32
            )

    def stats(p, i):
        rows, cols = pl.ds(i * 128, 128), part_cols(p)
        h = hidden[rows, cols] + delta_rows[rows, cols]
        hidden[rows, cols] = h
        gh = gain[:, cols] * h
        s1 = jnp.sum(h * h, axis=1, keepdims=True)
        s2 = jnp.sum(gh * gh, axis=1, keepdims=True)
        s3 = jnp.sum(gh * target[rows, cols].astype(F32), axis=1, keepdims=True)
        lane = lax.broadcasted_iota(jnp.int32, (128, 128), 1)
        return jnp.where(lane == 0, s1, jnp.where(lane == 1, s2, s3))

    def early_stats():
        for i in range(4):
            stat_acc[i] = stats(0, i)

    to_slots(tok, tok_out)
    partials(0, 0)
    pl.semaphore_wait(barrier, 2 * (N_DP - 1))
    a2a_start(tok_out, feat, a2a_sem.at[0])
    first_sends(0)
    scal_send[...] = jnp.zeros_like(scal_send)
    slot_tenants()
    to_slots(target, tgt_out)
    a2a_start(tgt_out, tgt_slots, a2a_sem.at[2])
    ring_step(0, 1)
    ring_step(0, 2)
    a2a_wait(tok_out, feat, a2a_sem.at[0])
    low_rank(down, feat, 1.0, rank_part)
    ar_first(rank_part, rank_land, 0, 1)
    ring_step(0, 3)
    ar_second(rank_part, rank_land, rank_full, 0, 1)
    ring_step(0, 4)
    ar_wait(rank_full, 0, 1)
    lax.fori_loop(0, SLOTS // 256, deltas, 0)
    a2a_start(delta_out, back_slots, a2a_sem.at[1])
    ring_step(0, 5)
    partials(1, 0)
    first_sends(1)
    ring_step(0, 6)
    ring_step(1, 1)
    last_hop(0)
    ring_step(1, 2)
    ring_step(1, 3)
    y_finish(0)
    to_owners(0)
    ring_step(1, 4)
    ring_step(1, 5)
    a2a_wait(delta_out, back_slots, a2a_sem.at[1])
    scatter_rows()
    early_stats()
    ring_step(1, 6)
    spread_tenants(rank_full)
    last_hop(1)
    y_finish(1)

    for i in range(4):
        table = stat_acc[i] + stats(1, i)
        stat_send[4 * i : 4 * i + 4, :] = table.T[0:4, :]

    def stat_copy(d):
        return pltpu.make_async_remote_copy(
            src_ref=stat_send,
            dst_ref=stat_land.at[d - 1],
            send_sem=stat_sem.at[0, d - 1],
            recv_sem=stat_sem.at[1, d - 1],
            device_id=(dp, (ten + d) % N_TEN),
            device_id_type=MESH,
        )

    each_peer(lambda d: stat_copy(d).start())
    to_owners(1)
    each_peer(lambda d: stat_copy(d).wait())

    total = stat_send[...]
    for d in range(N_TEN - 1):
        total = total + stat_land[d]
    invs, dots = [], []
    for i in range(4):
        s1, s2, s3 = (total[4 * i + q : 4 * i + q + 1, :] for q in range(3))
        inv = lax.rsqrt(s1 / MODEL_WIDTH + 1e-05)
        invs.append(inv)
        dots.append(inv * (inv * s2 - s3) / (8.0 * MODEL_WIDTH))

    pieces = []
    for rest in (jnp.concatenate(invs, axis=1), jnp.concatenate(dots, axis=1)):
        for _ in range(3):
            piece = rest.astype(BF).astype(F32)
            pieces.append(piece)
            rest = rest - piece
    pieces.append(jnp.zeros((10, ROWS), F32))
    placed = lax.dot_general(
        jnp.concatenate(pieces, axis=0).astype(BF),
        onehot[...],
        NT,
        preferred_element_type=F32,
    )
    pair = jnp.concatenate(
        [
            placed[0:1] + placed[1:2] + placed[2:3],
            placed[3:4] + placed[4:5] + placed[5:6],
        ],
        axis=0,
    )
    for d in range(N_DP):
        scal_send[d, 0:2, 0:CAP] = pair[:, d * CAP : (d + 1) * CAP]

    def scal_copy(d):
        peer = (dp + d) % N_DP
        return pltpu.make_async_remote_copy(
            src_ref=scal_send.at[peer],
            dst_ref=scal_land.at[dp],
            send_sem=scal_sem.at[0, d - 1],
            recv_sem=scal_sem.at[1, d - 1],
            device_id=(peer, ten),
            device_id_type=MESH,
        )

    each_peer(lambda d: scal_copy(d).start())
    scal_land[dp] = scal_send[dp]

    for i in range(4):
        rows = pl.ds(i * 128, 128)
        table = jnp.concatenate([invs[i], jnp.zeros((127, 128), F32)], axis=0).T
        inv = table[:, 0:1]
        draft[rows, :] = (hidden[rows, :] * inv * gain[...]).astype(BF)

    a2a_wait(tgt_out, tgt_slots, a2a_sem.at[2])
    for p in range(len(PHASES)):
        a2a_wait(h_out, h_slots, h_sem.at[p], part_cols(p))
    each_peer(lambda d: scal_copy(d).wait())

    def grads(s, carry):
        rows = slot_rows(s)
        table = jnp.concatenate([scal_land[s], jnp.zeros((120, 128), F32)], axis=0).T
        inv, dot = table[0:CAP, 0:1], table[0:CAP, 1:2]
        g = gain[...]
        h = h_slots[rows, :].astype(F32) + delta_out[rows, :].astype(F32)
        scaled = h * inv
        weighted = g * ((scaled * g - tgt_slots[rows, :].astype(F32)) / 8.0)
        gslots[rows, :] = (inv * (weighted - scaled * dot)).astype(BF)
        return carry

    for g, sources in enumerate(((0, 6), (6, 11), (11, N_DP))):
        lax.fori_loop(*sources, grads, 0)
        low_rank(up, gslots, 2.0, back_part, (2 * g, 2 * g + 2))
        ar_first(back_part, back_land, g, 3)
    for g in range(3):
        ar_second(back_part, back_land, back_full, g, 3)
    grouped_outer(gslots, 2.0, gup)
    for g in range(3):
        ar_wait(back_full, g, 3)
        spread_tenants(back_full, (2 * g, 2 * g + 2))
    grouped_outer(feat, 1.0, gdown)

    for p in range(len(PHASES)):
        for s in range(NZ - 1):

            def drain(i, carry, p=p, s=s):
                ring_copy(p, s, i).wait_send()
                return carry

            lax.fori_loop(0, 4, drain, 0)


def body(
    tokens,
    proj,
    gain,
    target,
    adapter_down_weight,
    adapter_up_weight,
    source_row_index,
    padded_row_index,
    padded_block_tenant,
):
    vmem = pl.BlockSpec(memory_space=pltpu.VMEM)
    wide = TEN * RANK
    dma = pltpu.SemaphoreType.DMA
    draft, grad_down, grad_up = pl.pallas_call(
        kernel,
        out_shape=(
            jax.ShapeDtypeStruct((ROWS, FEAT), BF),
            jax.ShapeDtypeStruct((wide, FEAT), BF),
            jax.ShapeDtypeStruct((wide, FEAT), BF),
        ),
        in_specs=[vmem, pl.BlockSpec(memory_space=pl.ANY)] + [vmem] * 7,
        out_specs=(vmem, vmem, vmem),
        scratch_shapes=[
            pltpu.VMEM((FEAT, MODEL_WIDTH), BF),
            pltpu.VMEM((SLOTS, ROWS), BF),
            pltpu.VMEM((SLOTS, FEAT), BF),
            pltpu.VMEM((SLOTS, FEAT), BF),
            pltpu.VMEM((SLOTS, FEAT), BF),
            pltpu.VMEM((SLOTS, FEAT), BF),
            pltpu.VMEM((SLOTS, FEAT), BF),
            pltpu.VMEM((SLOTS, FEAT), BF),
            pltpu.VMEM((SLOTS, FEAT), BF),
            pltpu.VMEM((SLOTS, FEAT), BF),
            pltpu.VMEM((SLOTS, FEAT), BF),
            pltpu.VMEM((256, wide), BF),
            pltpu.VMEM((wide, SLOTS), BF),
            pltpu.VMEM((2, 2, 256, FEAT), F32),
            pltpu.VMEM((4, 2, 128, FEAT), BF),
            pltpu.VMEM((NZ - 1, 4, 2, 128, FEAT), BF),
            pltpu.VMEM((4, 128, FEAT), BF),
            pltpu.VMEM((4, 128, FEAT), BF),
            pltpu.VMEM((ROWS, FEAT), F32),
            pltpu.VMEM((ROWS, FEAT), F32),
            pltpu.VMEM((ROWS, FEAT), BF),
            pltpu.VMEM((RANK, SLOTS), BF),
            pltpu.VMEM((N_TEN - 1, 16, LANES), BF),
            pltpu.VMEM((RANK, SLOTS), BF),
            pltpu.VMEM((RANK, SLOTS), BF),
            pltpu.VMEM((N_TEN - 1, 16, LANES), BF),
            pltpu.VMEM((RANK, SLOTS), BF),
            pltpu.VMEM((1, SLOTS), F32),
            pltpu.VMEM((SLOTS, 128), F32),
            pltpu.VMEM((4, 128, 128), F32),
            pltpu.VMEM((16, 128), F32),
            pltpu.VMEM((N_TEN - 1, 16, 128), F32),
            pltpu.VMEM((N_DP, 8, 128), F32),
            pltpu.VMEM((N_DP, 8, 128), F32),
            dma((NZ,)),
            dma((3, 2, N_DP - 1)),
            dma((len(PHASES), 2, N_DP - 1)),
            dma((2, N_DP - 1)),
            dma((2, len(PHASES), NZ - 1, 4)),
            dma((5, 4, N_TEN - 1)),
            dma((2, len(PHASES), 4)),
            dma((2, N_TEN - 1)),
        ],
        compiler_params=pltpu.CompilerParams(
            collective_id=0, has_side_effects=True, vmem_limit_bytes=58 << 20
        ),
        name="step",
    )(
        tokens,
        proj,
        gain.reshape(1, FEAT),
        target,
        adapter_down_weight.reshape(wide, FEAT),
        adapter_up_weight.reshape(wide, FEAT),
        source_row_index,
        padded_row_index,
        padded_block_tenant,
    )
    return (
        draft,
        grad_down.reshape(TEN, RANK, FEAT),
        grad_up.reshape(TEN, RANK, FEAT),
    )


def solution(mesh):
    return jax.shard_map(
        body,
        mesh=mesh,
        in_specs=(
            P("dp", "tensor"),
            P("tensor", None),
            P("tensor"),
            P("dp", "tensor"),
            P("dp", None, "tensor"),
            P("dp", None, "tensor"),
            P("dp", None, None),
            P("dp", None),
            P("dp", None),
        ),
        out_specs=(P("dp", "tensor"), P("dp", None, "tensor"), P("dp", None, "tensor")),
        check_vma=False,
    )
```

time: 171 us -> 161 us (0.942)
  Pallas kernels: 163 us -> 153 us
    pallas_call x1, Pallas kernels: 163 us -> 153 us  [body(): pl.pallas_call(kernel, out_shape=(jax.ShapeDtypeStruct((ROWS, FEAT), BF),...]
where the time goes in v3:
time: 161 us; the launch traced here: 160 us
  Pallas kernels  153 us (95%)
  local copies, waits for them, and re-layouts  6.44 us (4%)
    pallas_call x1, Pallas kernels, body(): pl.pallas_call(kernel, out_shape=(jax.ShapeDtypeStruct((ROWS, FEAT), BF),...  153 us
    unnamed x3, local copies, waits for them, and re-layouts  6.44 us

profile of v3, /device:TPU:4, one launch (start us, length us, event | category | flops | bytes accessed | tf_op | source)
XLA Modules:
  0.0 159.8 jit_solution(552737301290328099)
XLA Ops:
  0.6 152.7 %step.1 = (bf16[512,512]{1,0:T(8,128)(2,1)}, bf16[1024,512]{1,0:T(8,128)(2,1)}, bf16[1024,512]{1,0:T(8,128)(2,1)}) custom-call(bf16[512,512]{1,0:T(8,128)(2,1)} %tok.1, bf16[512,8192]{1,0:T(8,128)(2,1)} %proj.1, f32[1,512]{1,0:T(1,128)} %bitcast.9, bf16[512,512]{1,0:T(8,128)(2,1)} %target.1, bf16[1024,512]{1,0:T(8,128)(2,1)} %bitcast.5, ...), custom_call_target="tpu_custom_call" | custom-call | tf_op jit(solution)/shard_map/step/pallas_call | solution.py:555
  153.3 1.9 %copy.15 = bf16[512,512]{1,0:T(8,128)(2,1)} copy(bf16[512,512]{1,0:T(8,128)(2,1)} %get-tuple-element.12) | data formatting | bytes 1048576
  155.2 2.3 %copy.16 = bf16[16,64,512]{2,1,0:T(8,128)(2,1)} copy(bf16[16,64,512]{2,1,0:T(8,128)(2,1)} %bitcast.8) | data formatting | bytes 2097152
  157.5 2.3 %copy.17 = bf16[16,64,512]{2,1,0:T(8,128)(2,1)} copy(bf16[16,64,512]{2,1,0:T(8,128)(2,1)} %bitcast.7) | data formatting | bytes 2097152

commit v4 on v3

--- a/solution.py
+++ b/solution.py
@@ -31,13 +31,13 @@
 
 def kernel(
     tok, proj, gain, target, down, up, routes, positions, blocks,
-    draft, gdown, gup,
-    proj_v, onehot, tok_out, tgt_out, delta_out, h_out, feat, tgt_slots,
+    draft_out, gdown_out, gup_out,
+    draft, gdown, gup, proj_v, onehot, tok_out, tgt_out, delta_out, h_out, feat, tgt_slots,
     back_slots, h_slots, gslots, expand, expand_t,
     part, first, ring, ysend, yrecv, hidden, delta_rows, h_rows,
     rank_part, rank_land, rank_full, back_part, back_land, back_full,
     trow, tcol, stat_acc, stat_send, stat_land, scal_send, scal_land,
-    proj_sem, a2a_sem, h_sem, scal_sem, ring_sem, ar_sem, y_sem, stat_sem,
+    out_sem, proj_sem, a2a_sem, h_sem, scal_sem, ring_sem, ar_sem, y_sem, stat_sem,
 ):
     dp = lax.axis_index("dp")
     ten = lax.axis_index("tensor")
@@ -311,13 +311,15 @@
 
         lax.fori_loop(*tiles, one, 0)
 
-    def grouped_outer(rows_ref, scale, out):
+    def grouped_outer(rows_ref, scale, out, after=None):
         def one(t, carry):
             rows = pl.ds(aligned(t * 256, 256), 256)
             out[rows, :] = (
                 scale
                 * jnp.dot(expand_t[rows, :], rows_ref[...], preferred_element_type=F32)
             ).astype(BF)
+            if after:
+                after(t).start()
             return carry
 
         lax.fori_loop(0, TEN * RANK // 256, one, 0)
@@ -499,6 +501,8 @@
         table = jnp.concatenate([invs[i], jnp.zeros((127, 128), F32)], axis=0).T
         inv = table[:, 0:1]
         draft[rows, :] = (hidden[rows, :] * inv * gain[...]).astype(BF)
+    store_draft = pltpu.make_async_copy(draft, draft_out, out_sem.at[0])
+    store_draft.start()
 
     a2a_wait(tgt_out, tgt_slots, a2a_sem.at[2])
     for p in range(len(PHASES)):
@@ -523,10 +527,19 @@
     for g in range(3):
         ar_second(back_part, back_land, back_full, g, 3)
     grouped_outer(gslots, 2.0, gup)
+    store_up = pltpu.make_async_copy(gup, gup_out, out_sem.at[1])
+    store_up.start()
     for g in range(3):
         ar_wait(back_full, g, 3)
         spread_tenants(back_full, (2 * g, 2 * g + 2))
-    grouped_outer(feat, 1.0, gdown)
+
+    def store_down(t):
+        rows = pl.ds(aligned(t * 256, 256), 256)
+        return pltpu.make_async_copy(
+            gdown.at[rows, :], gdown_out.at[rows, :], out_sem.at[2 + t]
+        )
+
+    grouped_outer(feat, 1.0, gdown, store_down)
 
     for p in range(len(PHASES)):
         for s in range(NZ - 1):
@@ -536,6 +549,30 @@
                 return carry
 
             lax.fori_loop(0, 4, drain, 0)
+
+    store_draft.wait()
+    store_up.wait()
+    for t in range(4):
+        store_down(t).wait()
+
+
+def hand_on(*refs):
+    sems = refs[-1]
+    copies = []
+    for k in range(3):
+        src, dst = refs[k], refs[3 + k]
+        size = src.shape[0] // 4
+        for q in range(4):
+            rows = pl.ds(q * size, size)
+            copies.append(
+                pltpu.make_async_copy(
+                    src.at[rows, :], dst.at[rows, :], sems.at[4 * k + q]
+                )
+            )
+    for copy in copies:
+        copy.start()
+    for copy in copies:
+        copy.wait()
 
 
 def body(
@@ -550,18 +587,23 @@
     padded_block_tenant,
 ):
     vmem = pl.BlockSpec(memory_space=pltpu.VMEM)
+    hbm = pl.BlockSpec(memory_space=pl.ANY)
     wide = TEN * RANK
     dma = pltpu.SemaphoreType.DMA
-    draft, grad_down, grad_up = pl.pallas_call(
+    results = (
+        jax.ShapeDtypeStruct((ROWS, FEAT), BF),
+        jax.ShapeDtypeStruct((wide, FEAT), BF),
+        jax.ShapeDtypeStruct((wide, FEAT), BF),
+    )
+    made = pl.pallas_call(
         kernel,
-        out_shape=(
-            jax.ShapeDtypeStruct((ROWS, FEAT), BF),
-            jax.ShapeDtypeStruct((wide, FEAT), BF),
-            jax.ShapeDtypeStruct((wide, FEAT), BF),
-        ),
-        in_specs=[vmem, pl.BlockSpec(memory_space=pl.ANY)] + [vmem] * 7,
-        out_specs=(vmem, vmem, vmem),
+        out_shape=results,
+        in_specs=[vmem, hbm] + [vmem] * 7,
+        out_specs=(hbm, hbm, hbm),
         scratch_shapes=[
+            pltpu.VMEM((ROWS, FEAT), BF),
+            pltpu.VMEM((wide, FEAT), BF),
+            pltpu.VMEM((wide, FEAT), BF),
             pltpu.VMEM((FEAT, MODEL_WIDTH), BF),
             pltpu.VMEM((SLOTS, ROWS), BF),
             pltpu.VMEM((SLOTS, FEAT), BF),
@@ -596,6 +638,7 @@
             pltpu.VMEM((N_TEN - 1, 16, 128), F32),
             pltpu.VMEM((N_DP, 8, 128), F32),
             pltpu.VMEM((N_DP, 8, 128), F32),
+            dma((6,)),
             dma((NZ,)),
             dma((3, 2, N_DP - 1)),
             dma((len(PHASES), 2, N_DP - 1)),
@@ -620,6 +663,15 @@
         padded_row_index,
         padded_block_tenant,
     )
+    draft, grad_down, grad_up = pl.pallas_call(
+        hand_on,
+        out_shape=results,
+        in_specs=[hbm] * 3,
+        out_specs=(hbm,) * 3,
+        scratch_shapes=[dma((12,))],
+        compiler_params=pltpu.CompilerParams(vmem_limit_bytes=8 << 20),
+        name="hand_on",
+    )(*made)
     return (
         draft,
         grad_down.reshape(TEN, RANK, FEAT),

time: 161 us -> 158 us (0.981)
  local copies, waits for them, and re-layouts: 6.44 us -> 3.48 us
    unnamed x3 -> x6, local copies, waits for them, and re-layouts: 6.44 us -> 3.48 us
    pallas_call x1 -> x2, Pallas kernels: 153 us -> 153 us  [the longest x1 151 us: body(): pl.pallas_call(kernel, out_shape=results, in_specs=[vmem, hbm] + [vmem] *...]
where the time goes in v4:
time: 158 us; the launch traced here: 157 us
  Pallas kernels  153 us (97%)
  local copies, waits for them, and re-layouts  3.48 us (2%)
    pallas_call x1, Pallas kernels, body(): pl.pallas_call(kernel, out_shape=results, in_specs=[vmem, hbm] + [vmem] *...  151 us
    unnamed x6, local copies, waits for them, and re-layouts  3.48 us

profile of v4, /device:TPU:4, one launch (start us, length us, event | category | flops | bytes accessed | tf_op | source)
XLA Modules:
  0.0 156.9 jit_solution(536697583875063436)
XLA Ops:
  0.6 151.2 %step.1 = (bf16[512,512]{1,0:T(8,128)(2,1)}, bf16[1024,512]{1,0:T(8,128)(2,1)}, bf16[1024,512]{1,0:T(8,128)(2,1)}) custom-call(bf16[512,512]{1,0:T(8,128)(2,1)} %tok.1, bf16[512,8192]{1,0:T(8,128)(2,1)} %proj.1, f32[1,512]{1,0:T(1,128)} %bitcast.7, bf16[512,512]{1,0:T(8,128)(2,1)} %target.1, bf16[1024,512]{1,0:T(8,128)(2,1)} %bitcast.5, ...), custom_call_target="tpu_custom_call" | custom-call | tf_op jit(solution)/shard_map/step/pallas_call | solution.py:598
  151.8 0.0 copy-start
  151.8 1.2 copy-done
  153.0 0.0 copy-start.1
  153.0 1.2 copy-done.1
  154.2 0.0 copy-start.2
  154.2 1.0 copy-done.2
  155.3 1.6 %hand_on.1 = (bf16[512,512]{1,0:T(8,128)(2,1)}, bf16[1024,512]{1,0:T(8,128)(2,1)}, bf16[1024,512]{1,0:T(8,128)(2,1)}) custom-call(bf16[512,512]{1,0:T(8,128)(2,1)S(1)} %copy-done.2, bf16[1024,512]{1,0:T(8,128)(2,1)S(1)} %copy-done, bf16[1024,512]{1,0:T(8,128)(2,1)S(1)} %copy-done.1), custom_call_target="tpu_custom_call" | custom-call | tf_op jit(solution)/shard_map/hand_on/pallas_call | solution.py:666
Async XLA Ops:
  151.8 1.2 copy-start
  153.0 1.2 copy-start.1
  154.2 1.0 copy-start.2

commit v5 on v4

--- a/solution.py
+++ b/solution.py
@@ -103,11 +103,11 @@
         )
 
     def each_peer(action):
-        def one(d, carry):
-            action(d)
-            return carry
-
-        lax.fori_loop(1, N_TEN, one, 0)
+        def one(k, carry):
+            action(N_TEN // 2 + (1 - 2 * (k % 2)) * ((k + 1) // 2))
+            return carry
+
+        lax.fori_loop(0, N_TEN - 1, one, 0)
 
     def a2a_start(src, dst, sems, cols=everything):
         each_peer(lambda d: a2a_copy(src, dst, sems, cols, d).start())

time: 158 us -> 155 us (0.981)
  Pallas kernels: 153 us -> 150 us
    pallas_call x1, Pallas kernels: 151 us -> 148 us  [body(): pl.pallas_call(kernel, out_shape=results, in_specs=[vmem, hbm] + [vmem] *...]
where the time goes in v5:
time: 155 us; the launch traced here: 154 us
  Pallas kernels  150 us (97%)
  local copies, waits for them, and re-layouts  3.48 us (2%)
    pallas_call x1, Pallas kernels, body(): pl.pallas_call(kernel, out_shape=results, in_specs=[vmem, hbm] + [vmem] *...  148 us
    unnamed x6, local copies, waits for them, and re-layouts  3.48 us

profile of v5, /device:TPU:4, one launch (start us, length us, event | category | flops | bytes accessed | tf_op | source)
XLA Modules:
  0.0 154.1 jit_solution(16077377959349161929)
XLA Ops:
  0.6 148.2 %step.1 = (bf16[512,512]{1,0:T(8,128)(2,1)}, bf16[1024,512]{1,0:T(8,128)(2,1)}, bf16[1024,512]{1,0:T(8,128)(2,1)}) custom-call(bf16[512,512]{1,0:T(8,128)(2,1)} %tok.1, bf16[512,8192]{1,0:T(8,128)(2,1)} %proj.1, f32[1,512]{1,0:T(1,128)} %bitcast.7, bf16[512,512]{1,0:T(8,128)(2,1)} %target.1, bf16[1024,512]{1,0:T(8,128)(2,1)} %bitcast.5, ...), custom_call_target="tpu_custom_call" | custom-call | tf_op jit(solution)/shard_map/step/pallas_call | solution.py:598
  148.8 0.0 copy-start
  148.8 1.2 copy-done
  150.1 0.0 copy-start.1
  150.1 1.2 copy-done.1
  151.3 0.0 copy-start.2
  151.3 1.0 copy-done.2
  152.3 1.6 %hand_on.1 = (bf16[512,512]{1,0:T(8,128)(2,1)}, bf16[1024,512]{1,0:T(8,128)(2,1)}, bf16[1024,512]{1,0:T(8,128)(2,1)}) custom-call(bf16[512,512]{1,0:T(8,128)(2,1)S(1)} %copy-done.2, bf16[1024,512]{1,0:T(8,128)(2,1)S(1)} %copy-done, bf16[1024,512]{1,0:T(8,128)(2,1)S(1)} %copy-done.1), custom_call_target="tpu_custom_call" | custom-call | tf_op jit(solution)/shard_map/hand_on/pallas_call | solution.py:666
Async XLA Ops:
  148.8 1.2 copy-start
  150.1 1.2 copy-start.1
  151.3 1.0 copy-start.2
